TPU v7x, 32 devices: a whole 2x2x4 slice. The times are simulated.
32 devices in a mesh: runs: 2 (over y), tile: 4 (over z), layer: 2 (over x), star: 2 (over core).
Axes of the slice: x: 2, y: 2, z: 4, core: 2. Of those that a mesh axis runs over, the one named last changes fastest.
Arguments:
- screens: float32 [12, 384, 1536], P(('runs', 'layer'), 'tile'), parts along dimension 0, may hold values from -6 to 6
- layer_weight: float32 [12], P(('runs', 'layer')), parts along dimension 0, may hold values from 0.3 to 1
- wind_row: int32 [12], P('runs'), parts along dimension 0, may hold values from -4 to 4, as said below
- wind_col: int32 [12], P('runs'), parts along dimension 0, may hold values from -4 to 4, as said below
- foot_row: int32 [6, 6], replicated, may hold values from -80 to 79, as said below
- foot_col: int32 [6, 6], replicated, may hold values from -80 to 79, as said below
- frac_row: float32 [6, 6], replicated, may hold values from 0 to 1
- frac_col: float32 [6, 6], replicated, may hold values from 0 to 1
- amplitude: float32 [384, 1536], P('tile', 'layer'), may hold values from 0.5 to 2
- valid: int32 [24, 96], P('tile', 'layer'), may hold values 0 or 1
- recon_matrix: bfloat16 [6, 2, 24, 96, 2688], P('star', None, 'tile', 'layer'), may hold values from -0.0390625 to 0.0390625
- prev_recon: float32 [5376], P('runs'), parts along dimension 0, may hold values from -6 to 6
Outputs:
- shifted: float32 [12, 384, 1536], P(('runs', 'layer'), 'tile'), parts along dimension 0
- slopes: float32 [12, 2, 24, 96], P(('runs', 'star'), None, 'tile', 'layer'), parts along dimension 0
- commands: float32 [5376], P('runs'), parts along dimension 0
There are 2 independent parts, one for each index of `runs`. A program takes and returns all parts, laid end to end along the dimension named above; an argument that names none is the same for every part. Nothing has to cross between parts.
Inputs may be any that keep to these rules, and one draw needn't show every extreme that they name: `wind_row`: some layer takes 4 and another takes -4. `wind_col`: some layer takes 4 and another takes -4. `foot_row`: some star and layer take -80 and another takes 80 - 1. `foot_col`: some star and layer take -80 and another takes 80 - 1.
All inputs are finite; a program needn't handle non-finite values. No bound on the sum of `valid` on one device may be relied on, other than what follows from the above.
Results may differ from a plain program's by a relative error of at most 0.0019.
Values sent between devices are 32-bit elements; how exact they have to be, the bound alone decides.
A program may use at most 64 MiB of HBM per device.

v0:
```python
import functools
import math

import jax
import jax.numpy as jnp
import numpy as np
from jax import lax
from jax.experimental import pallas as pl
from jax.experimental.pallas import tpu as pltpu
from jax.sharding import PartitionSpec as P

PIX = 16
PAD = 32
WIND = 4
FOOT = 80
LANES = 128
HALO = -(-(WIND + FOOT + 1) // 8) * 8
MESH = pl.DeviceIdType.MESH
ANY = pl.BlockSpec(memory_space=pl.ANY)
SMEM = pl.BlockSpec(memory_space=pltpu.SMEM)
VMEM = pl.BlockSpec(memory_space=pltpu.VMEM)


def greet(peers):
    barrier = pltpu.get_barrier_semaphore()
    for peer in peers:
        pl.semaphore_signal(barrier, inc=1, device_id=peer, device_id_type=MESH)
    pl.semaphore_wait(barrier, len(peers))


def flow_kernel(
    tiles, cores, blocks, stars, weights, wind_row, wind_col, foot_row, foot_col,
    frac_row, frac_col, screens, share, shifted, field, land, outbox, inbox, zsend, zrecv, csend, crecv, xsend, xrecv, local,
):
    tile, core, layer = (lax.axis_index(n) for n in ("tile", "star", "layer"))
    up, down = lax.rem(tile + 1, tiles), lax.rem(tile + tiles - 1, tiles)
    partners = [lax.rem(core + k, cores) for k in range(1, cores)]
    peers = [lax.rem(layer + k, blocks) for k in range(1, blocks)]
    lays, rows, cols = screens.shape
    strips = cols // LANES
    per_block = strips // blocks
    unit = share.shape[2] // LANES // inbox.shape[1]
    units = inbox.shape[1]
    groups = rows // 8
    first = (layer + 1) * per_block + strips - 1
    star_start, layer_start = core * stars, layer * lays
    many = math.gcd(groups, 6)

    def column(n):
        return pl.ds(pl.multiple_of(lax.rem(first + n, strips) * LANES, LANES), LANES)

    copies = []
    for n in range(strips + 2):
        copy = pltpu.make_async_copy(
            screens.at[:, :, column(n % strips)],
            field.at[:, n, pl.ds(HALO, rows), :],
            local.at[n],
        )
        copy.start()
        copies.append(copy)
    greet(
        [{"tile": up}, {"tile": down}]
        + [{"star": p} for p in partners]
        + [{"layer": p} for p in peers]
    )
    sends = []
    for m in range(strips // cores):
        n = m * cores + core
        pair = []
        for d, (start, peer) in enumerate(((rows - HALO, up), (0, down))):
            copy = pltpu.make_async_remote_copy(
                src_ref=screens.at[:, pl.ds(start, HALO), column(n)],
                dst_ref=land.at[d, n],
                send_sem=zsend.at[m, d],
                recv_sem=zrecv.at[m, d],
                device_id={"tile": peer},
                device_id_type=MESH,
            )
            copy.start()
            pair.append(copy)
        sends.append(pair)
    for copy in copies:
        copy.wait()
    lane = lax.broadcasted_iota(jnp.int32, (8, LANES), 1)

    def window(j, row, base, n):
        return [field[j, base + n + k, pl.ds(row, 8), :] for k in range(unit + 1)]

    def place(start):
        base = start // LANES
        turn = start - base * LANES
        return base, turn

    def compute(u, store):
        low = u * unit

        def move_step(i, carry):
            for j in range(lays):
                base, turn = place(LANES - wind_col[layer_start + j])
                values = window(j, HALO + i * 8 - wind_row[layer_start + j], base, low)
                rolled = [pltpu.roll(v, (LANES - turn) & (LANES - 1), 1) for v in values]
                keep = lane < LANES - turn
                for k in range(unit):
                    shifted[j, pl.ds(pl.multiple_of(i * 8, 8), 8), column(low + k + 1)] = jnp.where(
                        keep, rolled[k], rolled[k + 1]
                    )
            return carry

        def pupil_step(n, carry):
            g = n // (groups // many)
            i = (n - g * (groups // many)) * many
            star = star_start + g
            total = [[None] * unit for _ in range(many)]
            for j in range(lays):
                lay = layer_start + j
                top_row = HALO + i * 8 + foot_row[star, lay] - wind_row[lay]
                base, turn = place(LANES + foot_col[star, lay] - wind_col[lay])
                weight = weights[j]
                a, b = frac_row[star, lay], frac_col[star, lay]
                top, bottom = weight * (1.0 - a), weight * a
                keep_near = lane < LANES - turn
                keep_far = lane < LANES - 1 - turn
                near_turn, far_turn = (LANES - turn) & (LANES - 1), LANES - 1 - turn
                for r in range(many):
                    row = top_row + r * 8
                    values = [
                        top * x + bottom * y
                        for x, y in zip(window(j, row, base, low), window(j, row + 1, base, low))
                    ]
                    near = [pltpu.roll(v, near_turn, 1) for v in values]
                    far = [pltpu.roll(v, far_turn, 1) for v in values]
                    for k in range(unit):
                        term = (1.0 - b) * jnp.where(
                            keep_near, near[k], near[k + 1]
                        ) + b * jnp.where(keep_far, far[k], far[k + 1])
                        total[r][k] = term if j == 0 else total[r][k] + term
            for r in range(many):
                for k in range(unit):
                    store(g, pl.ds(pl.multiple_of((i + r) * 8, 8), 8), k, total[r][k])
            return carry

        lax.fori_loop(0, stars * groups // many, pupil_step, 0)
        lax.fori_loop(0, groups, move_step, 0, unroll=math.gcd(groups, 3))

    def to_outbox(u):
        def store(g, at, k, value):
            outbox[u, g, at, k * LANES : (k + 1) * LANES] = value

        return store

    def to_share(u):
        def store(g, at, k, value):
            c = u * unit + k
            share[g, at, c * LANES : (c + 1) * LANES] = value

        return store

    forwards, swaps = [], []
    done = 0
    for m in range(strips // cores):
        n = m * cores + core
        current = []
        for d in range(2):
            sends[m][d].wait_recv()
            for k, p in enumerate(partners):
                forward = pltpu.make_async_remote_copy(
                    src_ref=land.at[d, n],
                    dst_ref=land.at[d, n],
                    send_sem=csend.at[m, d, k],
                    recv_sem=crecv.at[m, d, k],
                    device_id={"star": p},
                    device_id_type=MESH,
                )
                forward.start()
                current.append(forward)
        for forward in current:
            forward.wait_recv()
        forwards.extend(current)
        have = (m + 1) * cores
        for n in range(m * cores, have):
            for to in (n, n + strips):
                if to < strips + 2:
                    for j in range(lays):
                        field[j, to, 0:HALO, :] = land[0, n, j]
                        field[j, to, HALO + rows :, :] = land[1, n, j]
        while done < units * blocks and (
            have == strips or done * unit + unit + 2 <= have
        ):
            k, w = divmod(done, units)
            if k < blocks - 1:
                compute(done, to_outbox(done))
                copy = pltpu.make_async_remote_copy(
                    src_ref=outbox.at[done],
                    dst_ref=inbox.at[k, w],
                    send_sem=xsend.at[done],
                    recv_sem=xrecv.at[done],
                    device_id={"layer": peers[k]},
                    device_id_type=MESH,
                )
                copy.start()
                swaps.append(copy)
            else:
                compute(done, to_share(w))
            done += 1
    for n, copy in enumerate(swaps):
        k, w = divmod(n, units)
        copy.wait_recv()
        at = slice(w * unit * LANES, (w + 1) * unit * LANES)
        for g in range(stars):
            share[g, :, at] = share[g, :, at] + inbox[k, w, g]
    for pair in sends:
        for copy in pair:
            copy.wait_send()
    for copy in forwards + swaps:
        copy.wait_send()


def flow(scalars, screens, stars):
    tiles, blocks, cores = (lax.axis_size(n) for n in ("tile", "layer", "star"))
    lays, rows, cols = screens.shape
    strips = cols // LANES
    per_block = strips // blocks
    unit = 2 if per_block % 2 == 0 else 1
    units = per_block // unit
    width = cols // blocks
    steps = strips // cores
    dma = pltpu.SemaphoreType.DMA
    return pl.pallas_call(
        functools.partial(flow_kernel, tiles, cores, blocks, stars),
        out_shape=(
            jax.ShapeDtypeStruct((stars, rows, width), jnp.float32),
            jax.ShapeDtypeStruct((lays, rows, cols), jnp.float32),
        ),
        in_specs=[SMEM] * len(scalars) + [ANY],
        out_specs=(VMEM, VMEM),
        scratch_shapes=[
            pltpu.VMEM((lays, strips + 2, rows + 2 * HALO, LANES), jnp.float32),
            pltpu.VMEM((2, strips, lays, HALO, LANES), jnp.float32),
            pltpu.VMEM((units * (blocks - 1), stars, rows, unit * LANES), jnp.float32),
            pltpu.VMEM((blocks - 1, units, stars, rows, unit * LANES), jnp.float32),
            dma((steps, 2)),
            dma((steps, 2)),
            dma((steps, 2, cores - 1)),
            dma((steps, 2, cores - 1)),
            dma((units * (blocks - 1),)),
            dma((units * (blocks - 1),)),
            dma((strips + 2,)),
        ],
        compiler_params=pltpu.CompilerParams(collective_id=0, has_side_effects=True),
        name="flow",
    )(*scalars, screens)


def sine_cosine(x):
    turns = jnp.floor(x * (2.0 / math.pi) + 0.5)
    r = x - turns * 1.5703125
    r = r - turns * 4.837512969970703125e-4
    r = r - turns * 7.54978995489188216e-8
    z = r * r
    s = r + r * z * (-1.6666654611e-1 + z * (8.3321608736e-3 - z * 1.9515295891e-4))
    c = 1.0 - 0.5 * z + z * z * (
        4.166664568298827e-2 + z * (-1.388731625493765e-3 + z * 2.443315711809948e-5)
    )
    quadrant = turns.astype(jnp.int32)
    odd = (quadrant & 1) == 1
    sine = jnp.where(odd, c, s)
    cosine = jnp.where(odd, s, c)
    sine = jnp.where((quadrant & 2) == 2, -sine, sine)
    cosine = jnp.where(((quadrant + 1) & 2) == 2, -cosine, cosine)
    return sine, cosine


def halves(x):
    high = x.astype(jnp.bfloat16)
    return high, (x - high.astype(jnp.float32)).astype(jnp.bfloat16)


def product(x, y):
    return jnp.dot(x, y, preferred_element_type=jnp.float32)


def slope_kernel(
    share, amplitude, valid, row_high, row_low, row_alt, col_high, col_low, col_alt, gather,
    slopes, real, imag,
):
    stars, rows, cols = share.shape
    subs = rows // PIX

    def per_sub(values):
        return jnp.sum(values.reshape(subs, PIX, cols), axis=1)

    def collect(values):
        high, low = halves(values)
        return product(high, gather[...]) + product(low, gather[...])

    power = amplitude[...]
    scale = valid[...].astype(jnp.float32) / (collect(per_sub(power * power)) * PAD)
    for g in range(stars):

        def step(i, carry):
            at = pl.ds(pl.multiple_of(i * PIX, PIX), PIX)
            sine, cosine = sine_cosine(share[g, at, :])
            amp = amplitude[at, :]
            real[at, :] = amp * cosine
            imag[at, :] = amp * sine
            return carry

        lax.fori_loop(0, subs, step, 0)
        a, b = real[...], imag[...]
        a_high, a_low = halves(a)
        b_high, b_low = halves(b)
        turned = (
            product(row_high[...], b_high)
            + product(row_high[...], b_low)
            + product(row_low[...], b_high)
        )
        alt_a = (product(row_alt[...], a_high) + product(row_alt[...], a_low))[:subs]
        alt_b = (product(row_alt[...], b_high) + product(row_alt[...], b_low))[:subs]
        down = 2.0 * per_sub(a * turned) - PIX * (alt_a * alt_a + alt_b * alt_b)
        slopes[g, 0] = collect(down) * scale
        pieces = []
        for k in range(cols // LANES):
            at = slice(k * LANES, (k + 1) * LANES)
            turned = (
                product(b_high[:, at], col_high[...])
                + product(b_low[:, at], col_high[...])
                + product(b_high[:, at], col_low[...])
            )
            alt_a = product(a_high[:, at], col_alt[...]) + product(a_low[:, at], col_alt[...])
            alt_b = product(b_high[:, at], col_alt[...]) + product(b_low[:, at], col_alt[...])
            pieces.append(2.0 * a[:, at] * turned - (alt_a * alt_a + alt_b * alt_b))
        across = per_sub(jnp.concatenate(pieces, axis=1))
        slopes[g, 1] = collect(across) * scale


def tables(rows, cols):
    def block_diagonal(count, block):
        return np.kron(np.eye(count), block)

    index = np.arange(PIX)
    gap = index[:, None] - index[None, :]
    angle = np.where(gap == 0, 1, gap) * (math.pi / PAD)
    sign = np.where(gap % 2 == 0, 1.0, -1.0)
    table = np.where(gap == 0, 0.0, PIX * sign * np.cos(angle) / np.sin(angle))
    alternate = np.where(index % 2 == 0, 1.0, -1.0)
    subs = rows // PIX
    row_table = block_diagonal(subs, table)
    row_alt = np.pad(block_diagonal(subs, alternate[None, :]), ((0, -subs % 8), (0, 0)))
    per = LANES // PIX
    spread = np.zeros((PIX, PIX))
    spread[:, 0] = 4.0 * alternate
    col_table = block_diagonal(per, table.T)
    col_alt = block_diagonal(per, spread)
    gather = block_diagonal(cols // PIX, np.ones((PIX, 1)))

    def split(t):
        high = t.astype(jnp.bfloat16)
        return high, (t - high.astype(np.float64)).astype(jnp.bfloat16)

    exact = [t.astype(jnp.bfloat16) for t in (row_alt, col_alt, gather)]
    parts = (*split(row_table), exact[0], *split(col_table), exact[1], exact[2])
    return tuple(jnp.asarray(t) for t in parts)


def slopes_of(share, amplitude, valid):
    stars, rows, cols = share.shape
    subs = valid.shape
    return pl.pallas_call(
        slope_kernel,
        out_shape=jax.ShapeDtypeStruct((stars, 2) + subs, jnp.float32),
        in_specs=[VMEM] * 10,
        out_specs=VMEM,
        scratch_shapes=[
            pltpu.VMEM((rows, cols), jnp.float32),
            pltpu.VMEM((rows, cols), jnp.float32),
        ],
        name="slopes",
    )(share, amplitude, valid, *tables(rows, cols))


def reduce_kernel(tiles, blocks, cores, terms, out, near, far, nsend, nrecv, fsend, frecv):
    tile, layer, core = (lax.axis_index(n) for n in ("tile", "layer", "star"))
    count = blocks * cores
    me = layer * cores + core
    near_peers = []
    for k in range(1, count):
        rank = lax.rem(me + k, count)
        near_peers.append({"layer": rank // cores, "star": lax.rem(rank, cores)})
    far_peers = [{"tile": lax.rem(tile + k, tiles)} for k in range(1, tiles)]
    greet(near_peers + far_peers)
    copies = []
    for k, peer in enumerate(near_peers):
        copy = pltpu.make_async_remote_copy(
            src_ref=terms,
            dst_ref=near.at[me],
            send_sem=nsend.at[k],
            recv_sem=nrecv.at[k],
            device_id=peer,
            device_id_type=MESH,
        )
        copy.start()
        copies.append(copy)
    near[me] = terms[...]
    for copy in copies:
        copy.wait()
    total = near[0]
    for k in range(1, count):
        total = total + near[k]
    far[tile] = total
    copies = []
    for k, peer in enumerate(far_peers):
        copy = pltpu.make_async_remote_copy(
            src_ref=far.at[tile],
            dst_ref=far.at[tile],
            send_sem=fsend.at[k],
            recv_sem=frecv.at[k],
            device_id=peer,
            device_id_type=MESH,
        )
        copy.start()
        copies.append(copy)
    for copy in copies:
        copy.wait()
    total = far[0]
    for k in range(1, tiles):
        total = total + far[k]
    out[...] = total


def reduce_all(terms):
    tiles, blocks, cores = (lax.axis_size(n) for n in ("tile", "layer", "star"))
    count = blocks * cores
    return pl.pallas_call(
        functools.partial(reduce_kernel, tiles, blocks, cores),
        out_shape=jax.ShapeDtypeStruct(terms.shape, jnp.float32),
        in_specs=[VMEM],
        out_specs=VMEM,
        scratch_shapes=[
            pltpu.VMEM((count,) + terms.shape, jnp.float32),
            pltpu.VMEM((tiles,) + terms.shape, jnp.float32),
            pltpu.SemaphoreType.DMA((count - 1,)),
            pltpu.SemaphoreType.DMA((count - 1,)),
            pltpu.SemaphoreType.DMA((tiles - 1,)),
            pltpu.SemaphoreType.DMA((tiles - 1,)),
        ],
        compiler_params=pltpu.CompilerParams(collective_id=2, has_side_effects=True),
        name="reduce",
    )(terms)


def body(
    screens,
    layer_weight,
    wind_row,
    wind_col,
    foot_row,
    foot_col,
    frac_row,
    frac_col,
    amplitude,
    valid,
    recon_matrix,
    prev_recon,
):
    stars = recon_matrix.shape[0]
    scalars = (layer_weight, wind_row, wind_col, foot_row, foot_col, frac_row, frac_col)
    share, shifted = flow(scalars, screens, stars)
    slopes = slopes_of(share, amplitude, valid)
    local_terms = jnp.dot(
        slopes.astype(jnp.bfloat16).reshape(1, -1),
        recon_matrix.reshape(-1, recon_matrix.shape[-1]),
        preferred_element_type=jnp.float32,
    )
    recon = reduce_all(local_terms)[0]
    commands = 2.0 * recon - prev_recon
    return (shifted, slopes, commands)


def solution(mesh):
    return jax.shard_map(
        body,
        mesh=mesh,
        in_specs=(
            P(("runs", "layer"), "tile", None),
            P(("runs", "layer")),
            P("runs"),
            P("runs"),
            P(),
            P(),
            P(),
            P(),
            P("tile", "layer"),
            P("tile", "layer"),
            P("star", None, "tile", "layer", None),
            P("runs"),
        ),
        out_specs=(
            P(("runs", "layer"), "tile", None),
            P(("runs", "star"), None, "tile", "layer"),
            P("runs"),
        ),
        check_vma=False,
    )
```

profile of v0, /device:TPU:0, one launch (start us, length us, event | category | flops | bytes accessed | tf_op | source)
XLA Modules:
  0.0 76.2 jit_solution(3798396382301831830)
XLA Ops:
  0.6 0.0 copy-start.2
  0.6 47.0 %flow.1 = (f32[3,96,768]{2,1,0:T(8,128)}, f32[3,96,1536]{2,1,0:T(8,128)}) custom-call(f32[3]{0:T(128)} %weights.1, s32[6]{0:T(128)} %wind_row.1, s32[6]{0:T(128)} %wind_col.1, s32[6,6]{1,0:T(8,128)} %foot_row.1, s32[6,6]{1,0:T(8,128)} %foot_col.1, f32[6,6]{1,0:T(8,128)} %frac_row.1, f32[6,6]{1,0:T(8,128)} %frac_col.1, f32[3,96,1536]{2,1,0:T(8,128)} %screens.1), custom_call_target="tpu_custom_call" | custom-call | tf_op jit(solution)/shard_map/flow/pallas_call | solution.py:228
  47.7 0.0 copy-start
  47.7 6.8 %slopes.1 = f32[3,2,6,48]{3,2,1,0:T(8,128)} custom-call(f32[3,96,768]{2,1,0:T(8,128)} %get-tuple-element.6.share, f32[96,768]{1,0:T(8,128)} %amplitude.1, s32[6,48]{1,0:T(8,128)} %valid.1, bf16[96,96]{1,0:T(8,128)(2,1)} %constant.16.clone.row_high, bf16[96,96]{1,0:T(8,128)(2,1)} %constant.17.clone.row_low, bf16[8,96]{1,0:T(8,128)(2,1)} %constant.18.clone.row_alt, ...), custom_call_target="tpu_custom_call" | custom-call | tf_op jit(solution)/shard_map/slopes/pallas_call | solution.py:368
  54.5 0.0 copy-start.1
  54.5 0.8 %convert_bitcast_fusion = bf16[3,2,6,48,1]{3,2,1,0,4:T(8,128)(2,1)S(1)} fusion(f32[3,2,6,48]{3,2,1,0:T(8,128)} %slopes.1), kind=kLoop, calls=%fused_computation.2 | loop fusion | flops 1728 | bytes 10368 | tf_op jit(solution)/shard_map/convert_element_type | solution.py:470
  55.3 5.9 %convolution_bitcast_fusion.terms = f32[1,2688]{1,0:T(1,128)} fusion(bf16[3,2,6,48,2688]{4,3,2,1,0:T(8,128)(2,1)} %param.29, bf16[3,2,6,48,1]{3,2,1,0,4:T(8,128)(2,1)S(1)} %convert_bitcast_fusion), kind=kOutput, calls=%fused_computation | convolution fusion | flops 9289728 | bytes 9303936 | tf_op jit(solution)/shard_map/dot_general | solution.py:469
  61.2 11.8 %reduce.3 = f32[1,2688]{1,0:T(1,128)} custom-call(f32[1,2688]{1,0:T(1,128)} %convolution_bitcast_fusion.terms), custom_call_target="tpu_custom_call" | custom-call | tf_op jit(solution)/shard_map/reduce/pallas_call | solution.py:433
  73.0 0.7 multiply_reduce_fusion
  73.7 0.0 copy-done.2
  73.7 0.6 sub.3
  74.3 0.0 copy-done.1
  74.4 0.6 copy.22
  75.0 0.0 copy-done
  75.0 1.2 %copy.28 = f32[3,96,1536]{2,1,0:T(8,128)} copy(f32[3,96,1536]{2,1,0:T(8,128)S(1)} %copy-done) | data formatting | bytes 3538944
Async XLA Ops:
  0.6 73.1 %copy-start.2 = (f32[2688]{0:T(1024)S(1)}, f32[2688]{0:T(1024)}, u32[]{:S(2)}) copy-start(f32[2688]{0:T(1024)} %param.30) | copy-start | bytes 32260
  47.7 27.3 %copy-start = (f32[3,96,1536]{2,1,0:T(8,128)S(1)}, f32[3,96,1536]{2,1,0:T(8,128)}, u32[]{:S(2)}) copy-start(f32[3,96,1536]{2,1,0:T(8,128)} %get-tuple-element.13) | copy-start | bytes 5308420
  54.5 19.9 %copy-start.1 = (f32[3,2,6,48]{3,2,1,0:T(8,128)S(1)}, f32[3,2,6,48]{3,2,1,0:T(8,128)}, u32[]{:S(2)}) copy-start(f32[3,2,6,48]{3,2,1,0:T(8,128)} %slopes.1) | copy-start | bytes 20740
where the time goes:
time: 76.6 us; the launch traced here: 76.2 us
  Pallas kernels  65.6 us (86%)
  matrix products  5.89 us (8%)
  other arithmetic  2.15 us (3%)
  local copies, waits for them, and re-layouts  1.83 us (2%)
    pallas_call x1, Pallas kernels, flow(): pl.pallas_call(functools.partial(flow_kernel, tiles, cores, blocks, stars...  47 us
    pallas_call x1, Pallas kernels, reduce_all(): pl.pallas_call(functools.partial(reduce_kernel, tiles, blocks, cores), ou...  11.8 us
    pallas_call x1, Pallas kernels, slopes_of(): pl.pallas_call(slope_kernel, out_shape=jax.ShapeDtypeStruct((stars, 2) +...  6.81 us
    dot_general x1, matrix products, body(): jnp.dot(slopes.astype(jnp.bfloat16).reshape(1, -1), recon_matrix.reshape(...  5.89 us
    unnamed x8, local copies, waits for them, and re-layouts  1.83 us

commit v1 on v0

v1 whole, which is shorter than its diff:
```python
import functools
import math

import jax
import jax.numpy as jnp
import numpy as np
from jax import lax
from jax.experimental import pallas as pl
from jax.experimental.pallas import tpu as pltpu
from jax.sharding import PartitionSpec as P

PIX = 16
PAD = 32
WIND = 4
FOOT = 80
LANES = 128
HALO = -(-(WIND + FOOT + 1) // 8) * 8
MESH = pl.DeviceIdType.MESH
ANY = pl.BlockSpec(memory_space=pl.ANY)
SMEM = pl.BlockSpec(memory_space=pltpu.SMEM)
VMEM = pl.BlockSpec(memory_space=pltpu.VMEM)


def greet(peers):
    barrier = pltpu.get_barrier_semaphore()
    for peer in peers:
        pl.semaphore_signal(barrier, inc=1, device_id=peer, device_id_type=MESH)
    pl.semaphore_wait(barrier, len(peers))


def plan(rows, cols, blocks):
    strips = cols // LANES
    per_block = strips // blocks
    unit = 2 if per_block % 2 == 0 else 1
    units = per_block // unit
    group = 1 if (unit * LANES // PIX) % 16 == 0 else units
    return strips, per_block, unit, units, group


def frame_kernel(
    tiles, cores, blocks, stars, weights, wind_row, wind_col, foot_row, foot_col,
    frac_row, frac_col, screens, amplitude, valid, matrix, row_table, col_table, gather, spread,
    shifted, slopes, recon,
    field, land, outbox, inbox, share, moved, amp, mask, weight, row_tab, col_tab, gath, spre,
    scale, real, real_high, real_low, imag_high, imag_low, sums, total_terms, near, far,
    zsend, zrecv, csend, crecv, xsend, xrecv, local, load, store, nsend, nrecv, fsend, frecv,
):
    tile, core, layer = (lax.axis_index(n) for n in ("tile", "star", "layer"))
    up, down = lax.rem(tile + 1, tiles), lax.rem(tile + tiles - 1, tiles)
    partners = [lax.rem(core + k, cores) for k in range(1, cores)]
    peers = [lax.rem(layer + k, blocks) for k in range(1, blocks)]
    count = blocks * cores
    me = layer * cores + core
    near_peers = []
    for k in range(1, count):
        rank = lax.rem(me + k, count)
        near_peers.append({"layer": rank // cores, "star": lax.rem(rank, cores)})
    far_peers = [{"tile": lax.rem(tile + k, tiles)} for k in range(1, tiles)]
    lays, rows, cols = screens.shape
    strips, per_block, unit, units, group = plan(rows, cols, blocks)
    chunks = units // group
    width = group * unit * LANES
    subs = rows // PIX
    groups = rows // 8
    first = (layer + 1) * per_block + strips - 1
    star_start, layer_start = core * stars, layer * lays
    many = math.gcd(groups, 6)
    pairs = 2 * stars
    taps = matrix.shape[3] // chunks

    def column(n, size=1):
        start = pl.multiple_of(lax.rem(first + n, strips) * LANES, LANES)
        return pl.ds(start, size * LANES)

    copies = []
    for n in range(strips + 2):
        copy = pltpu.make_async_copy(
            screens.at[:, :, column(n % strips)],
            field.at[:, n, pl.ds(HALO, rows), :],
            local.at[n],
        )
        copy.start()
        copies.append(copy)
    greet(near_peers + far_peers)
    sends = []
    for m in range(strips // cores):
        n = m * cores + core
        pair = []
        for d, (start, peer) in enumerate(((rows - HALO, up), (0, down))):
            copy = pltpu.make_async_remote_copy(
                src_ref=screens.at[:, pl.ds(start, HALO), column(n)],
                dst_ref=land.at[d, n],
                send_sem=zsend.at[m, d],
                recv_sem=zrecv.at[m, d],
                device_id={"tile": peer},
                device_id_type=MESH,
            )
            copy.start()
            pair.append(copy)
        sends.append(pair)
    loads = []
    for n, (source, target) in enumerate(
        ((amplitude, amp), (valid, mask), (row_table, row_tab), (col_table, col_tab),
         (gather, gath), (spread, spre))
    ):
        copy = pltpu.make_async_copy(source, target, load.at[n])
        copy.start()
        loads.append(copy)
    matrix_copies = []
    for w in range(chunks):
        copy = pltpu.make_async_copy(
            matrix.at[:, :, :, w * taps : (w + 1) * taps, :],
            weight.at[w, :, :, 0:subs, 0:taps, :],
            load.at[len(loads) + w],
        )
        copy.start()
        matrix_copies.append(copy)
    high_rows = weight.shape[3]
    if high_rows > subs:
        for w in range(chunks):
            for g in range(stars):
                for d in range(2):
                    weight[w, g, d, subs:, :, :] = jnp.zeros(
                        (high_rows - subs,) + weight.shape[4:], weight.dtype
                    )
    if weight.shape[4] > taps:
        for w in range(chunks):
            for g in range(stars):
                for d in range(2):
                    weight[w, g, d, 0:subs, taps:, :] = jnp.zeros(
                        (subs, weight.shape[4] - taps, weight.shape[5]), weight.dtype
                    )
    sums[...] = jnp.zeros_like(sums)
    scale[...] = jnp.zeros_like(scale)

    def per_sub(values):
        return jnp.sum(values.reshape(subs, PIX, values.shape[1]), axis=1)

    def collect(values):
        high, low = halves(values)
        return product(high, gath[...]) + product(low, gath[...])

    for copy in loads:
        copy.wait()
    for w in range(chunks):
        power = amp[:, w * width : (w + 1) * width]
        sums[0:subs, :] = per_sub(power * power)
        lit = product(mask[...].astype(jnp.float32).astype(jnp.bfloat16), spre[w])
        scale[w, 0:subs, :] = lit / (collect(sums[0:8, :])[0:subs] * PAD)
    for copy in copies:
        copy.wait()
    lane = lax.broadcasted_iota(jnp.int32, (8, LANES), 1)

    def window(j, row, base, n):
        return [field[j, base + n + k, pl.ds(row, 8), :] for k in range(unit + 1)]

    def place(start):
        base = start // LANES
        turn = start - base * LANES
        return base, turn

    moves = []

    def move(u):
        low = u * unit

        def move_step(i, carry):
            for j in range(lays):
                base, turn = place(LANES - wind_col[layer_start + j])
                values = window(j, HALO + i * 8 - wind_row[layer_start + j], base, low)
                rolled = [pltpu.roll(v, (LANES - turn) & (LANES - 1), 1) for v in values]
                keep = lane < LANES - turn
                for k in range(unit):
                    moved[u, j, pl.ds(pl.multiple_of(i * 8, 8), 8), k * LANES : (k + 1) * LANES] = (
                        jnp.where(keep, rolled[k], rolled[k + 1])
                    )
            return carry

        lax.fori_loop(0, groups, move_step, 0, unroll=math.gcd(groups, 3))
        copy = pltpu.make_async_copy(
            moved.at[u], shifted.at[:, :, column(low + 1, unit)], store.at[u]
        )
        copy.start()
        moves.append(copy)

    def compute(u, put):
        low = u * unit

        def pupil_step(n, carry):
            g = n // (groups // many)
            i = (n - g * (groups // many)) * many
            star = star_start + g
            total = [[None] * unit for _ in range(many)]
            for j in range(lays):
                lay = layer_start + j
                top_row = HALO + i * 8 + foot_row[star, lay] - wind_row[lay]
                base, turn = place(LANES + foot_col[star, lay] - wind_col[lay])
                gain = weights[j]
                a, b = frac_row[star, lay], frac_col[star, lay]
                top, bottom = gain * (1.0 - a), gain * a
                keep_near = lane < LANES - turn
                keep_far = lane < LANES - 1 - turn
                near_turn, far_turn = (LANES - turn) & (LANES - 1), LANES - 1 - turn
                for r in range(many):
                    row = top_row + r * 8
                    values = [
                        top * x + bottom * y
                        for x, y in zip(window(j, row, base, low), window(j, row + 1, base, low))
                    ]
                    close = [pltpu.roll(v, near_turn, 1) for v in values]
                    beside = [pltpu.roll(v, far_turn, 1) for v in values]
                    for k in range(unit):
                        term = (1.0 - b) * jnp.where(
                            keep_near, close[k], close[k + 1]
                        ) + b * jnp.where(keep_far, beside[k], beside[k + 1])
                        total[r][k] = term if j == 0 else total[r][k] + term
            for r in range(many):
                for k in range(unit):
                    put(g, pl.ds(pl.multiple_of((i + r) * 8, 8), 8), k, total[r][k])
            return carry

        lax.fori_loop(0, stars * groups // many, pupil_step, 0)

    def to_outbox(u):
        def put(g, at, k, value):
            outbox[u, g, at, k * LANES : (k + 1) * LANES] = value

        return put

    def to_share(w):
        def put(g, at, k, value):
            share[w, g, at, k * LANES : (k + 1) * LANES] = value

        return put

    block = col_tab.shape[1]

    def slope_chunk(w):
        left = w * width

        def field_step(n, carry):
            g = n // subs
            i = n - g * subs
            at = pl.ds(pl.multiple_of(i * PIX, PIX), PIX)
            parts = []
            for v in range(w * group, (w + 1) * group):
                phase = share[v, g, at, :]
                for k in range(blocks - 1):
                    phase = phase + inbox[k, v, g, at, :]
                parts.append(phase)
            sine, cosine = sine_cosine(jnp.concatenate(parts, axis=1))
            power = amp[at, left : left + width]
            a, b = power * cosine, power * sine
            to = pl.ds(pl.multiple_of(n * PIX, PIX), PIX)
            real[to, :] = a
            real_high[to, :], real_low[to, :] = halves(a)
            imag_high[to, :], imag_low[to, :] = halves(b)
            return carry

        lax.fori_loop(0, stars * subs, field_step, 0)
        for g in range(stars):
            at = slice(g * rows, (g + 1) * rows)
            a = real[at, :]
            a_high, a_low = real_high[at, :], real_low[at, :]
            b_high, b_low = imag_high[at, :], imag_low[at, :]
            row_high, row_low, row_alt = (
                row_tab[0:rows, :], row_tab[rows : 2 * rows, :], row_tab[2 * rows :, :]
            )
            turned = product(row_high, b_high) + product(row_high, b_low) + product(row_low, b_high)
            alt_a = (product(row_alt, a_high) + product(row_alt, a_low))[:subs]
            alt_b = (product(row_alt, b_high) + product(row_alt, b_low))[:subs]
            along = 2.0 * per_sub(a * turned) - PIX * (alt_a * alt_a + alt_b * alt_b)
            sums[16 * g : 16 * g + subs, :] = along
            pieces = []
            for k in range(width // block):
                cut = slice(k * block, (k + 1) * block)
                turned = (
                    product(b_high[:, cut], col_tab[0])
                    + product(b_low[:, cut], col_tab[0])
                    + product(b_high[:, cut], col_tab[1])
                )
                alt_a = product(a_high[:, cut], col_tab[2]) + product(a_low[:, cut], col_tab[2])
                alt_b = product(b_high[:, cut], col_tab[2]) + product(b_low[:, cut], col_tab[2])
                pieces.append(2.0 * a[:, cut] * turned - (alt_a * alt_a + alt_b * alt_b))
            across = per_sub(jnp.concatenate(pieces, axis=1))
            sums[16 * g + 8 : 16 * g + 8 + subs, :] = across
        found = collect(sums[...])
        depth = weight.shape[4]
        mine = (
            lax.broadcasted_iota(jnp.int32, (8, found.shape[1]), 1) // depth
            == lax.broadcasted_iota(jnp.int32, (8, found.shape[1]), 0)
        )
        terms = []
        for n in range(pairs):
            part = found[8 * n : 8 * n + 8] * scale[w]
            g, d = divmod(n, 2)
            slopes[g, d, :, w * taps : (w + 1) * taps] = part[0:subs, 0:taps]
            terms.append(jnp.where(mine, part, 0.0).astype(jnp.bfloat16))
        matrix_copies[w].wait()
        left_side = jnp.concatenate(terms, axis=1)
        right_side = weight[w].reshape(left_side.shape[1], weight.shape[5])
        partial = jnp.dot(left_side, right_side, preferred_element_type=jnp.float32)
        partial = jnp.sum(partial, axis=0, keepdims=True)
        if w == 0:
            total_terms[...] = partial
        else:
            total_terms[...] = total_terms[...] + partial

    forwards, swaps = [], []
    done = 0
    late = []
    for m in range(strips // cores):
        n = m * cores + core
        current = []
        for d in range(2):
            sends[m][d].wait_recv()
            for k, p in enumerate(partners):
                forward = pltpu.make_async_remote_copy(
                    src_ref=land.at[d, n],
                    dst_ref=land.at[d, n],
                    send_sem=csend.at[m, d, k],
                    recv_sem=crecv.at[m, d, k],
                    device_id={"star": p},
                    device_id_type=MESH,
                )
                forward.start()
                current.append(forward)
        for forward in current:
            forward.wait_recv()
        forwards.extend(current)
        have = (m + 1) * cores
        for n in range(m * cores, have):
            for to in (n, n + strips):
                if to < strips + 2:
                    for j in range(lays):
                        field[j, to, 0:HALO, :] = land[0, n, j]
                        field[j, to, HALO + rows :, :] = land[1, n, j]
        while done < units * blocks and (
            have == strips or done * unit + unit + 2 <= have
        ):
            k, w = divmod(done, units)
            if k < blocks - 1:
                compute(done, to_outbox(done))
                copy = pltpu.make_async_remote_copy(
                    src_ref=outbox.at[done],
                    dst_ref=inbox.at[k, w],
                    send_sem=xsend.at[done],
                    recv_sem=xrecv.at[done],
                    device_id={"layer": peers[k]},
                    device_id_type=MESH,
                )
                copy.start()
                swaps.append(copy)
            else:
                compute(done, to_share(w))
                for q, copy in enumerate(swaps):
                    if q % units == w:
                        copy.wait_recv()
                if (w + 1) % group == 0:
                    slope_chunk(w // group)
            if have < strips:
                move(done)
            else:
                late.append(done)
            done += 1
    near_copies = []
    for k, peer in enumerate(near_peers):
        copy = pltpu.make_async_remote_copy(
            src_ref=total_terms,
            dst_ref=near.at[me],
            send_sem=nsend.at[k],
            recv_sem=nrecv.at[k],
            device_id=peer,
            device_id_type=MESH,
        )
        copy.start()
        near_copies.append(copy)
    near[me] = total_terms[...]
    for u in late:
        move(u)
    for copy in near_copies:
        copy.wait_recv()
    total = near[0]
    for k in range(1, count):
        total = total + near[k]
    far[tile] = total
    far_copies = []
    for k, peer in enumerate(far_peers):
        copy = pltpu.make_async_remote_copy(
            src_ref=far.at[tile],
            dst_ref=far.at[tile],
            send_sem=fsend.at[k],
            recv_sem=frecv.at[k],
            device_id=peer,
            device_id_type=MESH,
        )
        copy.start()
        far_copies.append(copy)
    for pair in sends:
        for copy in pair:
            copy.wait_send()
    for copy in forwards + swaps + near_copies:
        copy.wait_send()
    for copy in moves:
        copy.wait()
    for copy in far_copies:
        copy.wait()
    total = far[0]
    for k in range(1, tiles):
        total = total + far[k]
    recon[...] = total


def tables(rows, width, block, subs, taps, depth, chunks, high_rows):
    def block_diagonal(count, piece):
        return np.kron(np.eye(count), piece)

    index = np.arange(PIX)
    gap = index[:, None] - index[None, :]
    angle = np.where(gap == 0, 1, gap) * (math.pi / PAD)
    sign = np.where(gap % 2 == 0, 1.0, -1.0)
    table = np.where(gap == 0, 0.0, PIX * sign * np.cos(angle) / np.sin(angle))
    alternate = np.where(index % 2 == 0, 1.0, -1.0)
    row_part = block_diagonal(subs, table)
    row_alt = np.pad(block_diagonal(subs, alternate[None, :]), ((0, -subs % 16), (0, 0)))
    first = np.zeros((PIX, PIX))
    first[:, 0] = 4.0 * alternate
    col_part = block_diagonal(block // PIX, table.T)
    col_alt = block_diagonal(block // PIX, first)

    def split(t):
        high = np.asarray(t.astype(jnp.bfloat16), np.float64)
        return high, t - high

    row_all = np.concatenate([*split(row_part), row_alt], axis=0)
    col_all = np.stack([*split(col_part), col_alt])
    fold = np.zeros((taps, high_rows, depth))
    for k in range(taps):
        fold[k, :, k] = 1.0
    fold = fold.reshape(taps, high_rows * depth)
    gather = np.repeat(fold, PIX, axis=0)
    spread = np.zeros((chunks, chunks * taps, high_rows * depth))
    for w in range(chunks):
        spread[w, w * taps : (w + 1) * taps] = fold
    return tuple(jnp.asarray(t.astype(jnp.bfloat16)) for t in (row_all, col_all, gather, spread))


def frame(scalars, screens, amplitude, valid, matrix):
    tiles, blocks, cores = (lax.axis_size(n) for n in ("tile", "layer", "star"))
    lays, rows, cols = screens.shape
    stars, _, subs, sub_cols, commands = matrix.shape
    strips, per_block, unit, units, group = plan(rows, cols, blocks)
    chunks = units // group
    width = group * unit * LANES
    taps = sub_cols // chunks
    depth = -(-taps // 16) * 16
    high_rows = -(-subs // 8) * 8
    block = 2 * LANES if width % (2 * LANES) == 0 else LANES
    consts = tables(rows, width, block, subs, taps, depth, chunks, high_rows)
    count = blocks * cores
    steps = strips // cores
    dma = pltpu.SemaphoreType.DMA
    bf16, f32 = jnp.bfloat16, jnp.float32
    piece = (stars, rows, unit * LANES)
    return pl.pallas_call(
        functools.partial(frame_kernel, tiles, cores, blocks, stars),
        out_shape=(
            jax.ShapeDtypeStruct((lays, rows, cols), f32),
            jax.ShapeDtypeStruct((stars, 2, subs, sub_cols), f32),
            jax.ShapeDtypeStruct((1, commands), f32),
        ),
        in_specs=[SMEM] * len(scalars) + [ANY] * (4 + len(consts)),
        out_specs=(ANY, VMEM, VMEM),
        scratch_shapes=[
            pltpu.VMEM((lays, strips + 2, rows + 2 * HALO, LANES), f32),
            pltpu.VMEM((2, strips, lays, HALO, LANES), f32),
            pltpu.VMEM((units * (blocks - 1),) + piece, f32),
            pltpu.VMEM((blocks - 1, units) + piece, f32),
            pltpu.VMEM((units,) + piece, f32),
            pltpu.VMEM((units * blocks, lays, rows, unit * LANES), f32),
            pltpu.VMEM(amplitude.shape, f32),
            pltpu.VMEM(valid.shape, valid.dtype),
            pltpu.VMEM((chunks, stars, 2, high_rows, depth, commands), bf16),
        ]
        + [pltpu.VMEM(t.shape, bf16) for t in consts]
        + [
            pltpu.VMEM((chunks, 8, high_rows * depth), f32),
            pltpu.VMEM((stars * rows, width), f32),
            pltpu.VMEM((stars * rows, width), bf16),
            pltpu.VMEM((stars * rows, width), bf16),
            pltpu.VMEM((stars * rows, width), bf16),
            pltpu.VMEM((stars * rows, width), bf16),
            pltpu.VMEM((2 * stars * 8, width), f32),
            pltpu.VMEM((1, commands), f32),
            pltpu.VMEM((count, 1, commands), f32),
            pltpu.VMEM((tiles, 1, commands), f32),
            dma((steps, 2)),
            dma((steps, 2)),
            dma((steps, 2, cores - 1)),
            dma((steps, 2, cores - 1)),
            dma((units * (blocks - 1),)),
            dma((units * (blocks - 1),)),
            dma((strips + 2,)),
            dma((6 + chunks,)),
            dma((units * blocks,)),
            dma((count - 1,)),
            dma((count - 1,)),
            dma((tiles - 1,)),
            dma((tiles - 1,)),
        ],
        compiler_params=pltpu.CompilerParams(collective_id=0, has_side_effects=True),
        name="frame",
    )(*scalars, screens, amplitude, valid, matrix, *consts)


def sine_cosine(x):
    turns = jnp.floor(x * (2.0 / math.pi) + 0.5)
    r = x - turns * 1.5703125
    r = r - turns * 4.837512969970703125e-4
    r = r - turns * 7.54978995489188216e-8
    z = r * r
    s = r + r * z * (-1.6666654611e-1 + z * (8.3321608736e-3 - z * 1.9515295891e-4))
    c = 1.0 - 0.5 * z + z * z * (
        4.166664568298827e-2 + z * (-1.388731625493765e-3 + z * 2.443315711809948e-5)
    )
    quadrant = turns.astype(jnp.int32)
    odd = (quadrant & 1) == 1
    sine = jnp.where(odd, c, s)
    cosine = jnp.where(odd, s, c)
    sine = jnp.where((quadrant & 2) == 2, -sine, sine)
    cosine = jnp.where(((quadrant + 1) & 2) == 2, -cosine, cosine)
    return sine, cosine


def halves(x):
    high = x.astype(jnp.bfloat16)
    return high, (x - high.astype(jnp.float32)).astype(jnp.bfloat16)


def product(x, y):
    return jnp.dot(x, y, preferred_element_type=jnp.float32)


def body(
    screens,
    layer_weight,
    wind_row,
    wind_col,
    foot_row,
    foot_col,
    frac_row,
    frac_col,
    amplitude,
    valid,
    recon_matrix,
    prev_recon,
):
    scalars = (layer_weight, wind_row, wind_col, foot_row, foot_col, frac_row, frac_col)
    shifted, slopes, recon = frame(scalars, screens, amplitude, valid, recon_matrix)
    commands = 2.0 * recon[0] - prev_recon
    return (shifted, slopes, commands)


def solution(mesh):
    return jax.shard_map(
        body,
        mesh=mesh,
        in_specs=(
            P(("runs", "layer"), "tile", None),
            P(("runs", "layer")),
            P("runs"),
            P("runs"),
            P(),
            P(),
            P(),
            P(),
            P("tile", "layer"),
            P("tile", "layer"),
            P("star", None, "tile", "layer", None),
            P("runs"),
        ),
        out_specs=(
            P(("runs", "layer"), "tile", None),
            P(("runs", "star"), None, "tile", "layer"),
            P("runs"),
        ),
        check_vma=False,
    )
```

time: 76.6 us -> 67.6 us (0.88)
  matrix products: 5.89 us -> 0 us
  Pallas kernels: 65.6 us -> 61.2 us
  local copies, waits for them, and re-layouts: 1.83 us -> 4.15 us
  other arithmetic: 2.15 us -> 1.34 us
    dot_general x1 -> x0, matrix products: 5.89 us -> none  [body(): jnp.dot(slopes.astype(jnp.bfloat16).reshape(1, -1), recon_matrix.reshape(...]
    pallas_call x3 -> x1, Pallas kernels: 65.6 us -> 61.2 us  [frame(): pl.pallas_call(functools.partial(frame_kernel, tiles, cores, blocks, star...]
    unnamed x8 -> x4, local copies, waits for them, and re-layouts: 1.83 us -> 4.15 us
    convert_element_type x1 -> x0, other arithmetic: 0.81 us -> none  [body(): slopes.astype(jnp.bfloat16).reshape(1, -1)]
where the time goes in v1:
time: 67.6 us; the launch traced here: 67.3 us
  Pallas kernels  61.2 us (91%)
  local copies, waits for them, and re-layouts  4.15 us (6%)
  other arithmetic  1.34 us (2%)
    pallas_call x1, Pallas kernels, frame(): pl.pallas_call(functools.partial(frame_kernel, tiles, cores, blocks, star...  61.2 us
    unnamed x4, local copies, waits for them, and re-layouts  4.15 us

profile of v1, /device:TPU:0, one launch (start us, length us, event | category | flops | bytes accessed | tf_op | source)
XLA Modules:
  0.0 67.3 jit_solution(5182954749185540352)
XLA Ops:
  0.6 0.0 copy-start
  0.6 61.2 %frame.1 = (f32[3,96,1536]{2,1,0:T(8,128)}, f32[3,2,6,48]{3,2,1,0:T(8,128)}, f32[1,2688]{1,0:T(1,128)}) custom-call(f32[3]{0:T(128)} %weights.1, s32[6]{0:T(128)} %wind_row.1, s32[6]{0:T(128)} %wind_col.1, s32[6,6]{1,0:T(8,128)} %foot_row.1, s32[6,6]{1,0:T(8,128)} %foot_col.1, f32[6,6]{1,0:T(8,128)} %frac_row.1, f32[6,6]{1,0:T(8,128)} %frac_col.1, ...), custom_call_target="tpu_custom_call" | custom-call | tf_op jit(solution)/shard_map/frame/pallas_call | solution.py:465
  61.8 0.7 %multiply_reduce_fusion = f32[2688]{0:T(1024)S(1)} fusion(f32[1,2688]{1,0:T(1,128)} %get-tuple-element.8), kind=kLoop, calls=%fused_computation | loop fusion | flops 2688 | bytes 21504 | tf_op jit(solution)/shard_map/mul | solution.py:560
  62.6 0.0 copy-done
  62.6 0.6 sub.3
  63.2 1.4 %copy.19 = f32[3,2,6,48]{3,1,2,0:T(2,128)} copy(f32[3,2,6,48]{3,2,1,0:T(8,128)} %get-tuple-element.10) | data formatting | bytes 13824
  64.5 2.8 %copy.21 = f32[3,96,1536]{2,1,0:T(8,128)} copy(f32[3,96,1536]{2,1,0:T(8,128)} %get-tuple-element.15) | data formatting | bytes 3538944
Async XLA Ops:
  0.6 61.9 %copy-start = (f32[2688]{0:T(1024)S(1)}, f32[2688]{0:T(1024)}, u32[]{:S(2)}) copy-start(f32[2688]{0:T(1024)} %param.27) | copy-start | bytes 32260

commit v2 on v1

--- a/solution.py
+++ b/solution.py
@@ -17,6 +17,7 @@
 HALO = -(-(WIND + FOOT + 1) // 8) * 8
 MESH = pl.DeviceIdType.MESH
 ANY = pl.BlockSpec(memory_space=pl.ANY)
+HBM = pl.BlockSpec(memory_space=pltpu.HBM)
 SMEM = pl.BlockSpec(memory_space=pltpu.SMEM)
 VMEM = pl.BlockSpec(memory_space=pltpu.VMEM)
 
@@ -38,12 +39,13 @@
 
 
 def frame_kernel(
-    tiles, cores, blocks, stars, weights, wind_row, wind_col, foot_row, foot_col,
-    frac_row, frac_col, screens, amplitude, valid, matrix, row_table, col_table, gather, spread,
+    tiles, cores, blocks, stars, weights_in, wind_row_in, wind_col_in, foot_row_in, foot_col_in,
+    frac_row_in, frac_col_in, screens, amplitude, valid, matrix, row_table, col_table, gather, spread,
     shifted, slopes, recon,
-    field, land, outbox, inbox, share, moved, amp, mask, weight, row_tab, col_tab, gath, spre,
+    weights, wind_row, wind_col, foot_row, foot_col, frac_row, frac_col,
+    field, land, outbox, inbox, share, amp, mask, weight, row_tab, col_tab, gath, spre,
     scale, real, real_high, real_low, imag_high, imag_low, sums, total_terms, near, far,
-    zsend, zrecv, csend, crecv, xsend, xrecv, local, load, store, nsend, nrecv, fsend, frecv,
+    zsend, zrecv, csend, crecv, xsend, xrecv, local, load, nsend, nrecv, fsend, frecv,
 ):
     tile, core, layer = (lax.axis_index(n) for n in ("tile", "star", "layer"))
     up, down = lax.rem(tile + 1, tiles), lax.rem(tile + tiles - 1, tiles)
@@ -101,7 +103,9 @@
     loads = []
     for n, (source, target) in enumerate(
         ((amplitude, amp), (valid, mask), (row_table, row_tab), (col_table, col_tab),
-         (gather, gath), (spread, spre))
+         (gather, gath), (spread, spre), (weights_in, weights), (wind_row_in, wind_row),
+         (wind_col_in, wind_col), (foot_row_in, foot_row), (foot_col_in, foot_col),
+         (frac_row_in, frac_row), (frac_col_in, frac_col))
     ):
         copy = pltpu.make_async_copy(source, target, load.at[n])
         copy.start()
@@ -159,8 +163,6 @@
         turn = start - base * LANES
         return base, turn
 
-    moves = []
-
     def move(u):
         low = u * unit
 
@@ -171,17 +173,12 @@
                 rolled = [pltpu.roll(v, (LANES - turn) & (LANES - 1), 1) for v in values]
                 keep = lane < LANES - turn
                 for k in range(unit):
-                    moved[u, j, pl.ds(pl.multiple_of(i * 8, 8), 8), k * LANES : (k + 1) * LANES] = (
-                        jnp.where(keep, rolled[k], rolled[k + 1])
+                    shifted[j, pl.ds(pl.multiple_of(i * 8, 8), 8), column(low + k + 1)] = jnp.where(
+                        keep, rolled[k], rolled[k + 1]
                     )
             return carry
 
         lax.fori_loop(0, groups, move_step, 0, unroll=math.gcd(groups, 3))
-        copy = pltpu.make_async_copy(
-            moved.at[u], shifted.at[:, :, column(low + 1, unit)], store.at[u]
-        )
-        copy.start()
-        moves.append(copy)
 
     def compute(u, put):
         low = u * unit
@@ -294,7 +291,7 @@
         for n in range(pairs):
             part = found[8 * n : 8 * n + 8] * scale[w]
             g, d = divmod(n, 2)
-            slopes[g, d, :, w * taps : (w + 1) * taps] = part[0:subs, 0:taps]
+            slopes[g, :, d, w * taps : (w + 1) * taps] = part[0:subs, 0:taps]
             terms.append(jnp.where(mine, part, 0.0).astype(jnp.bfloat16))
         matrix_copies[w].wait()
         left_side = jnp.concatenate(terms, axis=1)
@@ -401,8 +398,6 @@
             copy.wait_send()
     for copy in forwards + swaps + near_copies:
         copy.wait_send()
-    for copy in moves:
-        copy.wait()
     for copy in far_copies:
         copy.wait()
     total = far[0]
@@ -443,6 +438,10 @@
     for w in range(chunks):
         spread[w, w * taps : (w + 1) * taps] = fold
     return tuple(jnp.asarray(t.astype(jnp.bfloat16)) for t in (row_all, col_all, gather, spread))
+
+
+def stay(*arrays):
+    return [pltpu.with_memory_space_constraint(x, pltpu.HBM) for x in arrays]
 
 
 def frame(scalars, screens, amplitude, valid, matrix):
@@ -465,19 +464,19 @@
     return pl.pallas_call(
         functools.partial(frame_kernel, tiles, cores, blocks, stars),
         out_shape=(
-            jax.ShapeDtypeStruct((lays, rows, cols), f32),
-            jax.ShapeDtypeStruct((stars, 2, subs, sub_cols), f32),
-            jax.ShapeDtypeStruct((1, commands), f32),
+            pltpu.VMEM((lays, rows, cols), f32),
+            pltpu.VMEM((stars, subs, 2, sub_cols), f32),
+            pltpu.VMEM((1, commands), f32),
         ),
-        in_specs=[SMEM] * len(scalars) + [ANY] * (4 + len(consts)),
-        out_specs=(ANY, VMEM, VMEM),
-        scratch_shapes=[
+        in_specs=[HBM] * (len(scalars) + 4 + len(consts)),
+        out_specs=(VMEM, VMEM, VMEM),
+        scratch_shapes=[pltpu.SMEM(t.shape, t.dtype) for t in scalars]
+        + [
             pltpu.VMEM((lays, strips + 2, rows + 2 * HALO, LANES), f32),
             pltpu.VMEM((2, strips, lays, HALO, LANES), f32),
             pltpu.VMEM((units * (blocks - 1),) + piece, f32),
             pltpu.VMEM((blocks - 1, units) + piece, f32),
             pltpu.VMEM((units,) + piece, f32),
-            pltpu.VMEM((units * blocks, lays, rows, unit * LANES), f32),
             pltpu.VMEM(amplitude.shape, f32),
             pltpu.VMEM(valid.shape, valid.dtype),
             pltpu.VMEM((chunks, stars, 2, high_rows, depth, commands), bf16),
@@ -501,16 +500,17 @@
             dma((units * (blocks - 1),)),
             dma((units * (blocks - 1),)),
             dma((strips + 2,)),
-            dma((6 + chunks,)),
-            dma((units * blocks,)),
+            dma((6 + len(scalars) + chunks,)),
             dma((count - 1,)),
             dma((count - 1,)),
             dma((tiles - 1,)),
             dma((tiles - 1,)),
         ],
-        compiler_params=pltpu.CompilerParams(collective_id=0, has_side_effects=True),
+        compiler_params=pltpu.CompilerParams(
+            collective_id=0, has_side_effects=True, vmem_limit_bytes=48 * 2**20
+        ),
         name="frame",
-    )(*scalars, screens, amplitude, valid, matrix, *consts)
+    )(*stay(*scalars, screens, amplitude, valid, matrix, *consts))
 
 
 def sine_cosine(x):
@@ -540,6 +540,32 @@
 def product(x, y):
     return jnp.dot(x, y, preferred_element_type=jnp.float32)
 
+def finish_kernel(moved, found, recon, previous, shifted, slopes, commands, sems):
+    copies = [
+        pltpu.make_async_copy(moved.at[j], shifted.at[j], sems.at[j]) for j in range(moved.shape[0])
+    ]
+    copies.append(pltpu.make_async_copy(found, slopes, sems.at[moved.shape[0]]))
+    for copy in copies:
+        copy.start()
+    commands[...] = 2.0 * recon[0, :] - previous[...]
+    for copy in copies:
+        copy.wait()
+
+
+def finish(moved, found, recon, previous):
+    shifted, slopes, commands = pl.pallas_call(
+        finish_kernel,
+        out_shape=tuple(
+            jax.ShapeDtypeStruct(x.shape, jnp.float32) for x in (moved, found, previous)
+        ),
+        in_specs=[ANY, ANY, VMEM, VMEM],
+        out_specs=(ANY, ANY, VMEM),
+        scratch_shapes=[pltpu.SemaphoreType.DMA((moved.shape[0] + 1,))],
+        compiler_params=pltpu.CompilerParams(vmem_limit_bytes=2**20),
+        name="finish",
+    )(moved, found, recon, previous)
+    return shifted, jnp.transpose(slopes, (0, 2, 1, 3)), commands
+
 
 def body(
     screens,
@@ -556,9 +582,8 @@
     prev_recon,
 ):
     scalars = (layer_weight, wind_row, wind_col, foot_row, foot_col, frac_row, frac_col)
-    shifted, slopes, recon = frame(scalars, screens, amplitude, valid, recon_matrix)
-    commands = 2.0 * recon[0] - prev_recon
-    return (shifted, slopes, commands)
+    moved, found, recon = frame(scalars, screens, amplitude, valid, recon_matrix)
+    return finish(moved, found, recon, prev_recon)
 
 
 def solution(mesh):

time: 67.6 us -> 62.3 us (0.922)
  local copies, waits for them, and re-layouts: 4.15 us -> 0.01 us
  other arithmetic: 1.34 us -> 0 us
    unnamed x4 -> x2, local copies, waits for them, and re-layouts: 4.15 us -> 0.01 us
    pallas_call x0 -> x1, Pallas kernels: none -> 1.84 us  [finish(): pl.pallas_call(finish_kernel, out_shape=tuple((jax.ShapeDtypeStruct(x.sha...]
    pallas_call x1, Pallas kernels: 61.2 us -> 59.7 us  [frame(): pl.pallas_call(functools.partial(frame_kernel, tiles, cores, blocks, star...]
    mul x1 -> x0, other arithmetic: 0.74 us -> none  [body(): commands = 2.0 * recon[0] - prev_recon]
where the time goes in v2:
time: 62.3 us; the launch traced here: 62.2 us
  Pallas kernels  61.5 us (99%)
  between operations  0.66 us (1%)
    pallas_call x1, Pallas kernels, frame(): pl.pallas_call(functools.partial(frame_kernel, tiles, cores, blocks, star...  59.7 us
    pallas_call x1, Pallas kernels, finish(): pl.pallas_call(finish_kernel, out_shape=tuple((jax.ShapeDtypeStruct(x.sha...  1.84 us

profile of v2, /device:TPU:0, one launch (start us, length us, event | category | flops | bytes accessed | tf_op | source)
XLA Modules:
  0.0 62.2 jit_solution(9967473407183877183)
XLA Ops:
  0.6 0.0 copy-start
  0.6 59.7 %frame.1 = (f32[3,96,1536]{2,1,0:T(8,128)S(1)}, f32[3,6,2,48]{3,2,1,0:T(2,128)S(1)}, f32[1,2688]{1,0:T(1,128)S(1)}) custom-call(f32[3]{0:T(128)} %weights_in.1, s32[6]{0:T(128)} %wind_row_in.1, s32[6]{0:T(128)} %wind_col_in.1, s32[6,6]{1,0:T(8,128)} %foot_row_in.1, s32[6,6]{1,0:T(8,128)} %foot_col_in.1, f32[6,6]{1,0:T(8,128)} %frac_row_in.1, ...), custom_call_target="tpu_custom_call" | custom-call | tf_op jit(solution)/shard_map/frame/pallas_call | solution.py:464
  60.3 0.0 copy-done
  60.3 1.8 %finish.1 = (f32[3,96,1536]{2,1,0:T(8,128)}, f32[3,6,2,48]{3,2,1,0:T(2,128)}, f32[2688]{0:T(1024)}) custom-call(f32[3,96,1536]{2,1,0:T(8,128)S(1)} %get-tuple-element.9.moved, f32[3,6,2,48]{3,2,1,0:T(2,128)S(1)} %get-tuple-element.10.found, f32[1,2688]{1,0:T(1,128)S(1)} %get-tuple-element.11.recon, f32[2688]{0:T(1024)S(1)} %copy-done), custom_call_target="tpu_custom_call" | custom-call | tf_op jit(solution)/shard_map/finish/pallas_call | solution.py:556
Async XLA Ops:
  0.6 59.7 %copy-start = (f32[2688]{0:T(1024)S(1)}, f32[2688]{0:T(1024)}, u32[]{:S(2)}) copy-start(f32[2688]{0:T(1024)} %previous.1) | copy-start | bytes 32260

commit v3 on v2

v3 whole, which is shorter than its diff:
```python
import functools
import math

import jax
import jax.numpy as jnp
import numpy as np
from jax import lax
from jax.experimental import pallas as pl
from jax.experimental.pallas import tpu as pltpu
from jax.sharding import PartitionSpec as P

PIX = 16
PAD = 32
WIND = 4
FOOT = 80
LANES = 128
HALO = -(-(WIND + FOOT + 1) // 8) * 8
MESH = pl.DeviceIdType.MESH
ANY = pl.BlockSpec(memory_space=pl.ANY)
HBM = pl.BlockSpec(memory_space=pltpu.HBM)
SMEM = pl.BlockSpec(memory_space=pltpu.SMEM)
VMEM = pl.BlockSpec(memory_space=pltpu.VMEM)


def greet(peers):
    barrier = pltpu.get_barrier_semaphore()
    for peer in peers:
        pl.semaphore_signal(barrier, inc=1, device_id=peer, device_id_type=MESH)
    pl.semaphore_wait(barrier, len(peers))


def plan(rows, cols, blocks):
    strips = cols // LANES
    per_block = strips // blocks
    unit = 2 if per_block % 2 == 0 else 1
    units = per_block // unit
    group = 1 if (unit * LANES // PIX) % 16 == 0 else units
    return strips, per_block, unit, units, group


def row_parts(rows):
    parts = 3 if (rows // PIX) % 3 == 0 else 1
    reach = WIND + FOOT + 1 - (rows // parts if parts > 1 else 0)
    return parts, min(HALO, -(-reach // 8) * 8)


def frame_kernel(
    tiles, cores, blocks, stars, weights_in, wind_row_in, wind_col_in, foot_row_in, foot_col_in,
    frac_row_in, frac_col_in, screens, amplitude, valid, matrix, row_table, col_table, gather, spread,
    shifted, slopes, recon,
    weights, wind_row, wind_col, foot_row, foot_col, frac_row, frac_col,
    field, land, outbox, inbox, share, amp, mask, weight, row_tab, col_tab, gath, spre,
    scale, amp_turned, real, stack, sums, total_terms, near, far,
    zsend, zrecv, csend, crecv, xsend, xrecv, local, load, nsend, nrecv, fsend, frecv,
):
    tile, core, layer = (lax.axis_index(n) for n in ("tile", "star", "layer"))
    up, down = lax.rem(tile + 1, tiles), lax.rem(tile + tiles - 1, tiles)
    partners = [lax.rem(core + k, cores) for k in range(1, cores)]
    peers = [lax.rem(layer + k, blocks) for k in range(1, blocks)]
    count = blocks * cores
    me = layer * cores + core
    near_peers = []
    for k in range(1, count):
        rank = lax.rem(me + k, count)
        near_peers.append({"layer": rank // cores, "star": lax.rem(rank, cores)})
    far_peers = [{"tile": lax.rem(tile + k, tiles)} for k in range(1, tiles)]
    lays, rows, cols = screens.shape
    strips, per_block, unit, units, group = plan(rows, cols, blocks)
    chunks = units // group
    width = group * unit * LANES
    subs = rows // PIX
    parts, inner = row_parts(rows)
    part_rows, part_subs = rows // parts, subs // parts
    first = (layer + 1) * per_block + strips - 1
    star_start, layer_start = core * stars, layer * lays
    groups = rows // 8
    many = groups // parts
    block_rows = stars * part_rows
    block_subs = stars * part_subs
    taps = matrix.shape[3] // chunks

    def column(n, size=1):
        start = pl.multiple_of(lax.rem(first + n, strips) * LANES, LANES)
        return pl.ds(start, size * LANES)

    copies = []
    for n in range(strips + 2):
        copy = pltpu.make_async_copy(
            screens.at[:, :, column(n % strips)],
            field.at[:, n, pl.ds(HALO, rows), :],
            local.at[n],
        )
        copy.start()
        copies.append(copy)
    greet(near_peers + far_peers)
    steps = strips // cores
    last = steps - 1
    pieces = [(m, d, 0, HALO) for m in range(last) for d in range(2)]
    near_rows = [(last, 0, HALO - inner, inner), (last, 1, 0, inner)]
    far_rows = [(last, 0, 0, HALO - inner), (last, 1, inner, HALO - inner)]
    far_rows = [p for p in far_rows if p[3]]
    pieces += near_rows + far_rows
    sends = []
    for q, (m, d, low, size) in enumerate(pieces):
        n = m * cores + core
        start, peer = ((rows - HALO, up), (0, down))[d]
        copy = pltpu.make_async_remote_copy(
            src_ref=screens.at[:, pl.ds(start + low, size), column(n)],
            dst_ref=land.at[d, n, :, pl.ds(low, size), :],
            send_sem=zsend.at[q],
            recv_sem=zrecv.at[q],
            device_id={"tile": peer},
            device_id_type=MESH,
        )
        copy.start()
        sends.append(copy)
    loads = []
    for n, (source, target) in enumerate(
        ((amplitude, amp), (valid, mask), (row_table, row_tab), (col_table, col_tab),
         (gather, gath), (spread, spre), (weights_in, weights), (wind_row_in, wind_row),
         (wind_col_in, wind_col), (foot_row_in, foot_row), (foot_col_in, foot_col),
         (frac_row_in, frac_row), (frac_col_in, frac_col))
    ):
        copy = pltpu.make_async_copy(source, target, load.at[n])
        copy.start()
        loads.append(copy)
    matrix_copies = []

    def fetch_matrix():
        for w in range(chunks):
            for p in range(parts):
                for d in range(2):
                    copy = pltpu.make_async_copy(
                        matrix.at[
                            :, d, p * part_subs : (p + 1) * part_subs, w * taps : (w + 1) * taps, :
                        ],
                        weight.at[w, p, d, 0:stars, :, 0:taps, :],
                        load.at[len(loads) + len(matrix_copies)],
                    )
                    copy.start()
                    matrix_copies.append(copy)

    slots, depth = weight.shape[3], weight.shape[5]
    for w in range(chunks):
        for p in range(parts):
            for d in range(2):
                if slots > stars:
                    weight[w, p, d, stars:] = jnp.zeros(
                        (slots - stars,) + weight.shape[4:], weight.dtype
                    )
                if depth > taps:
                    weight[w, p, d, 0:stars, :, taps:, :] = jnp.zeros(
                        (stars, part_subs, depth - taps, weight.shape[6]), weight.dtype
                    )
    scale[...] = jnp.zeros_like(scale)

    def per_sub(values):
        return jnp.sum(values.reshape(-1, PIX, values.shape[1]), axis=1)

    def collect(values):
        high, low = halves(values)
        return product(high, gath[...]) + product(low, gath[...])

    for copy in loads:
        copy.wait()
    amp_turned[...] = -amp[...]
    for w in range(chunks):
        power = amp[:, w * width : (w + 1) * width]
        total = per_sub(power * power)
        lit = product(mask[...].astype(jnp.float32).astype(jnp.bfloat16), spre[w])
        ratio = lit / (collect(total) * PAD)
        for p in range(parts):
            for d in range(2):
                for g in range(stars):
                    at = d * slots * part_subs + g * part_subs
                    scale[w, p, at : at + part_subs, :] = ratio[
                        p * part_subs : (p + 1) * part_subs
                    ]
    for copy in copies:
        copy.wait()
    lane = lax.broadcasted_iota(jnp.int32, (8, LANES), 1)

    def window(j, row, base, n):
        return [field[j, base + n + k, pl.ds(row, 8), :] for k in range(unit + 1)]

    def place(start):
        base = start // LANES
        turn = start - base * LANES
        return base, turn

    def move(u):
        low = u * unit

        def move_step(i, carry):
            for j in range(lays):
                base, turn = place(LANES - wind_col[layer_start + j])
                values = window(j, HALO + i * 8 - wind_row[layer_start + j], base, low)
                rolled = [pltpu.roll(v, (LANES - turn) & (LANES - 1), 1) for v in values]
                keep = lane < LANES - turn
                for k in range(unit):
                    shifted[j, pl.ds(pl.multiple_of(i * 8, 8), 8), column(low + k + 1)] = jnp.where(
                        keep, rolled[k], rolled[k + 1]
                    )
            return carry

        lax.fori_loop(0, groups, move_step, 0, unroll=math.gcd(groups, 3))

    def compute(u, put, chosen, unroll=1):
        low = u * unit

        def pupil_step(g, carry):
            star = star_start + g
            for part in chosen:
                plain = [[None] * unit for _ in range(many)]
                ahead = [[None] * (unit + 1) for _ in range(many)]
                for j in range(lays):
                    lay = layer_start + j
                    top_row = HALO + part * part_rows + foot_row[star, lay] - wind_row[lay]
                    base, turn = place(LANES + foot_col[star, lay] - wind_col[lay])
                    gain = weights[j]
                    a, b = frac_row[star, lay], frac_col[star, lay]
                    top, bottom = gain * (1.0 - a), gain * a
                    keep = lane < LANES - turn
                    back = (LANES - turn) & (LANES - 1)
                    for r in range(many):
                        row = top_row + r * 8
                        rolled = [
                            pltpu.roll(top * x + bottom * y, back, 1)
                            for x, y in zip(
                                window(j, row, base, low), window(j, row + 1, base, low)
                            )
                        ]
                        shift = [
                            jnp.where(keep, rolled[k], rolled[k + 1]) for k in range(unit)
                        ] + [rolled[unit]]
                        for k in range(unit):
                            term = (1.0 - b) * shift[k]
                            plain[r][k] = term if j == 0 else plain[r][k] + term
                        for k in range(unit + 1):
                            term = b * shift[k]
                            ahead[r][k] = term if j == 0 else ahead[r][k] + term
                for r in range(many):
                    beside = [pltpu.roll(v, LANES - 1, 1) for v in ahead[r]]
                    for k in range(unit):
                        value = plain[r][k] + jnp.where(
                            lane < LANES - 1, beside[k], beside[k + 1]
                        )
                        at = pl.ds(part * part_rows + r * 8, 8)
                        put(g, at, k, value)
            return carry

        lax.fori_loop(0, stars, pupil_step, 0, unroll=unroll)

    def to_outbox(u):
        def put(g, at, k, value):
            outbox[u, g, at, k * LANES : (k + 1) * LANES] = value

        return put

    def to_share(w):
        def put(g, at, k, value):
            share[w, g, at, k * LANES : (k + 1) * LANES] = value

        return put

    block = col_tab.shape[1]

    high_half = slots * part_subs

    def fields(slot, w, p):
        left = w * width
        for n in range(block_subs):
            g, i = divmod(n, part_subs)
            at = slice((p * part_subs + i) * PIX, (p * part_subs + i + 1) * PIX)
            strip = []
            for v in range(w * group, (w + 1) * group):
                phase = share[v, g, at, :]
                for k in range(blocks - 1):
                    phase = phase + inbox[k, v, g, at, :]
                strip.append(phase)
            sine, cosine, turns = sine_cosine(jnp.concatenate(strip, axis=1))
            power = jnp.where(
                (turns.astype(jnp.int32) & 1) == 1,
                amp_turned[at, left : left + width],
                amp[at, left : left + width],
            )
            a, b = power * cosine, power * sine
            real[slot, n * PIX : (n + 1) * PIX, :] = a
            for q, value in enumerate(halves(b) + halves(a)):
                low = q * block_rows + n * PIX
                stack[slot, low : low + PIX, :] = value

    def centroids(slot, w, p):
        a = real[slot]
        found = product(row_tab[...], stack[slot])
        turned = found[0:block_rows] + found[block_rows : 2 * block_rows]
        alt_a = found[2 * block_rows : 2 * block_rows + block_subs]
        step = (found.shape[0] - 2 * block_rows) // 2
        alt_b = found[2 * block_rows + step : 2 * block_rows + step + block_subs]
        sums[slot, 0:block_subs, :] = per_sub(a * turned) - PIX * (alt_a * alt_a + alt_b * alt_b)
        if high_half > block_subs:
            fill = jnp.zeros((high_half - block_subs, width), jnp.float32)
            sums[slot, block_subs:high_half, :] = fill
            sums[slot, high_half + block_subs :, :] = fill
        b_high, b_low, a_high, a_low = (
            stack[slot, q * block_rows : (q + 1) * block_rows, :] for q in range(4)
        )
        across = []
        for k in range(width // block):
            cut = slice(k * block, (k + 1) * block)
            turned = product(
                jnp.concatenate([b_high[:, cut], b_low[:, cut], b_high[:, cut]], axis=1),
                col_tab[0 : 3 * block, :],
            )
            alt = product(
                jnp.concatenate([x[:, cut] for x in (a_high, a_low, b_high, b_low)], axis=1),
                col_tab[3 * block :, :],
            )
            across.append(a[:, cut] * turned - alt * alt)
        sums[slot, high_half : high_half + block_subs, :] = per_sub(
            jnp.concatenate(across, axis=1)
        )
        found = collect(sums[slot]) * scale[w, p]
        for d in range(2):
            for g in range(stars):
                at = d * high_half + g * part_subs
                for i in range(part_subs):
                    slopes[g, p * part_subs + i, d : d + 1, w * taps : (w + 1) * taps] = found[
                        at + i : at + i + 1, w * depth : w * depth + taps
                    ]
        mine = (
            lax.broadcasted_iota(jnp.int32, found.shape, 1) // depth
            == lax.broadcasted_iota(jnp.int32, found.shape, 0)
        )
        return jnp.where(mine, found, 0.0).astype(jnp.bfloat16)

    def slope_parts(chosen):
        terms = []
        slots_here = real.shape[0]
        for n, (w, p) in enumerate(chosen):
            if n == 0:
                fields(0, w, p)
            if n + 1 < len(chosen):
                fields((n + 1) % slots_here, *chosen[n + 1])
            terms.append((w, p, centroids(n % slots_here, w, p)))
        return terms

    started = []

    def project(terms):
        for w, p, _ in terms:
            for d in range(2):
                matrix_copies[(w * parts + p) * 2 + d].wait()
        partial = None
        for w, p, left_side in terms:
            right_side = weight[w, p].reshape(left_side.shape[1], weight.shape[6])
            value = jnp.dot(left_side, right_side, preferred_element_type=jnp.float32)
            partial = value if partial is None else partial + value
        partial = jnp.sum(partial, axis=0, keepdims=True)
        if started:
            total_terms[...] = total_terms[...] + partial
        else:
            total_terms[...] = partial
            started.append(True)

    forwards, swaps = [], []

    passing = {}

    def send_on(chosen):
        for q in chosen:
            m, d, low, size = pieces[q]
            mine = land.at[d, m * cores + core, :, pl.ds(low, size), :]
            sends[q].wait_recv()
            passing[q] = []
            for k, p in enumerate(partners):
                forward = pltpu.make_async_remote_copy(
                    src_ref=mine,
                    dst_ref=mine,
                    send_sem=csend.at[q, k],
                    recv_sem=crecv.at[q, k],
                    device_id={"star": p},
                    device_id_type=MESH,
                )
                forward.start()
                passing[q].append(forward)

    def take(chosen):
        for q in chosen:
            for forward in passing[q]:
                forward.wait_recv()
                forwards.append(forward)
            m, d, low, size = pieces[q]
            base = low + d * (HALO + rows)
            for n in range(m * cores, (m + 1) * cores):
                for to in (n, n + strips):
                    if to < strips + 2:
                        for j in range(lays):
                            field[j, to, base : base + size, :] = land[d, n, j, low : low + size, :]

    def own(u, chosen, unroll=1):
        k, w = divmod(u, units)
        compute(u, to_share(w), chosen, unroll)

    def arrived(w):
        for q, copy in enumerate(swaps):
            if q % units == w:
                copy.wait_recv()

    whole = list(range(parts))
    done = 0
    for m in range(last):
        send_on([2 * m, 2 * m + 1])
        take([2 * m, 2 * m + 1])
        if m == 0:
            fetch_matrix()
        have = (m + 1) * cores
        while done < units * blocks and done * unit + unit + 2 <= have:
            k, w = divmod(done, units)
            if k < blocks - 1:
                compute(done, to_outbox(done), whole)
                copy = pltpu.make_async_remote_copy(
                    src_ref=outbox.at[done],
                    dst_ref=inbox.at[k, w],
                    send_sem=xsend.at[done],
                    recv_sem=xrecv.at[done],
                    device_id={"layer": peers[k]},
                    device_id_type=MESH,
                )
                copy.start()
                swaps.append(copy)
            else:
                own(done, whole)
                arrived(w)
                if (w + 1) % group == 0:
                    c = w // group
                    project(slope_parts([(c, p) for p in whole]))
            move(done)
            done += 1
    late = list(range(done, units * blocks))
    late_chunks = sorted({(u % units) // group for u in late})
    split = last * 2 + 2 < len(pieces)
    send_on([2 * last, 2 * last + 1])
    take([2 * last, 2 * last + 1])
    if split:
        outer = [2 * last + 2, 2 * last + 3]
        middle = whole[1:-1]
        for u in late:
            own(u, middle, True)
            arrived(u % units)
        terms = slope_parts([(c, p) for c in late_chunks for p in middle])
        send_on(outer)
        project(terms)
        take(outer)
    rest = [whole[0], whole[-1]] if split else whole
    for u in late:
        own(u, rest, True)
        if not split:
            arrived(u % units)
    project(slope_parts([(c, p) for c in late_chunks for p in rest]))
    near_copies = []
    for k, peer in enumerate(near_peers):
        copy = pltpu.make_async_remote_copy(
            src_ref=total_terms,
            dst_ref=near.at[me],
            send_sem=nsend.at[k],
            recv_sem=nrecv.at[k],
            device_id=peer,
            device_id_type=MESH,
        )
        copy.start()
        near_copies.append(copy)
    near[me] = total_terms[...]
    for u in late:
        move(u)
    for copy in near_copies:
        copy.wait_recv()
    total = near[0]
    for k in range(1, count):
        total = total + near[k]
    far[tile] = total
    far_copies = []
    for k, peer in enumerate(far_peers):
        copy = pltpu.make_async_remote_copy(
            src_ref=far.at[tile],
            dst_ref=far.at[tile],
            send_sem=fsend.at[k],
            recv_sem=frecv.at[k],
            device_id=peer,
            device_id_type=MESH,
        )
        copy.start()
        far_copies.append(copy)
    for copy in sends + forwards + swaps + near_copies:
        copy.wait_send()
    for copy in far_copies:
        copy.wait()
    total = far[0]
    for k in range(1, tiles):
        total = total + far[k]
    recon[...] = total


def tables(block, block_subs, taps, depth, chunks, lanes):
    def block_diagonal(count, piece):
        return np.kron(np.eye(count), piece)

    index = np.arange(PIX)
    gap = index[:, None] - index[None, :]
    angle = np.where(gap == 0, 1, gap) * (math.pi / PAD)
    sign = np.where(gap % 2 == 0, 1.0, -1.0)
    table = np.where(gap == 0, 0.0, PIX * sign * np.cos(angle) / np.sin(angle))
    alternate = np.where(index % 2 == 0, 1.0, -1.0)
    def split(t):
        high = np.asarray(t.astype(jnp.bfloat16), np.float64)
        return high, t - high

    row_high, row_low = split(block_diagonal(block_subs, 2.0 * table))
    row_alt = np.pad(block_diagonal(block_subs, alternate[None, :]), ((0, -block_subs % 16), (0, 0)))
    none, thin = np.zeros_like(row_high), np.zeros_like(row_alt)
    row_all = np.block([
        [row_high, row_high, none, none],
        [row_low, none, none, none],
        [thin, thin, row_alt, row_alt],
        [row_alt, row_alt, thin, thin],
    ])
    ends = np.zeros((2, PIX, PIX))
    for n in range(2):
        ends[n, :, n] = 4.0 * alternate
    count = block // PIX
    col_high, col_low = split(block_diagonal(count, 2.0 * table.T))
    alt_a, alt_b = (block_diagonal(count, end) for end in ends)
    col_all = np.concatenate([col_high, col_high, col_low, alt_a, alt_a, alt_b, alt_b], axis=0)
    fold = np.zeros((taps, lanes // depth, depth))
    for k in range(taps):
        fold[k, :, k] = 1.0
    fold = fold.reshape(taps, lanes)
    gather = np.repeat(fold, PIX, axis=0)
    spread = np.zeros((chunks, chunks * taps, lanes))
    for w in range(chunks):
        spread[w, w * taps : (w + 1) * taps] = fold
    return tuple(jnp.asarray(t.astype(jnp.bfloat16)) for t in (row_all, col_all, gather, spread))


def stay(*arrays):
    return [pltpu.with_memory_space_constraint(x, pltpu.HBM) for x in arrays]


def frame(scalars, screens, amplitude, valid, matrix):
    tiles, blocks, cores = (lax.axis_size(n) for n in ("tile", "layer", "star"))
    lays, rows, cols = screens.shape
    stars, _, subs, sub_cols, commands = matrix.shape
    strips, per_block, unit, units, group = plan(rows, cols, blocks)
    chunks = units // group
    width = group * unit * LANES
    taps = sub_cols // chunks
    depth = -(-taps // 16) * 16
    parts, inner = row_parts(rows)
    part_subs = subs // parts
    slots = stars
    while slots * part_subs % 8:
        slots += 1
    lanes = 2 * slots * part_subs * depth
    pieces = 2 * (strips // cores) + (2 if inner < HALO else 0)
    block = 2 * LANES if width % (2 * LANES) == 0 else LANES
    consts = tables(block, stars * part_subs, taps, depth, chunks, lanes)
    count = blocks * cores
    dma = pltpu.SemaphoreType.DMA
    bf16, f32 = jnp.bfloat16, jnp.float32
    piece = (stars, rows, unit * LANES)
    return pl.pallas_call(
        functools.partial(frame_kernel, tiles, cores, blocks, stars),
        out_shape=(
            pltpu.VMEM((lays, rows, cols), f32),
            pltpu.VMEM((stars, subs, 2, sub_cols), f32),
            pltpu.VMEM((1, commands), f32),
        ),
        in_specs=[HBM] * (len(scalars) + 4 + len(consts)),
        out_specs=(VMEM, VMEM, VMEM),
        scratch_shapes=[pltpu.SMEM(t.shape, t.dtype) for t in scalars]
        + [
            pltpu.VMEM((lays, strips + 2, rows + 2 * HALO, LANES), f32),
            pltpu.VMEM((2, strips, lays, HALO, LANES), f32),
            pltpu.VMEM((units * (blocks - 1),) + piece, f32),
            pltpu.VMEM((blocks - 1, units) + piece, f32),
            pltpu.VMEM((units,) + piece, f32),
            pltpu.VMEM(amplitude.shape, f32),
            pltpu.VMEM(valid.shape, valid.dtype),
            pltpu.VMEM((chunks, parts, 2, slots, part_subs, depth, commands), bf16),
        ]
        + [pltpu.VMEM(t.shape, bf16) for t in consts]
        + [
            pltpu.VMEM((chunks, parts, 2 * slots * part_subs, lanes), f32),
            pltpu.VMEM(amplitude.shape, f32),
            pltpu.VMEM((4, stars * rows // parts, width), f32),
            pltpu.VMEM((4, 4 * stars * rows // parts, width), bf16),
            pltpu.VMEM((4, 2 * slots * part_subs, width), f32),
            pltpu.VMEM((1, commands), f32),
            pltpu.VMEM((count, 1, commands), f32),
            pltpu.VMEM((tiles, 1, commands), f32),
            dma((pieces,)),
            dma((pieces,)),
            dma((pieces, cores - 1)),
            dma((pieces, cores - 1)),
            dma((units * (blocks - 1),)),
            dma((units * (blocks - 1),)),
            dma((strips + 2,)),
            dma((6 + len(scalars) + chunks * parts * 2,)),
            dma((count - 1,)),
            dma((count - 1,)),
            dma((tiles - 1,)),
            dma((tiles - 1,)),
        ],
        compiler_params=pltpu.CompilerParams(
            collective_id=0, has_side_effects=True, vmem_limit_bytes=48 * 2**20
        ),
        name="frame",
    )(*stay(*scalars, screens, amplitude, valid, matrix, *consts))


def horner(z, first, *rest):
    value = first
    for c in rest:
        value = value * z + c
    return value


def sine_cosine(x):
    turns = jnp.floor(x * (1.0 / math.pi) + 0.5)
    r = x - turns * 3.140625
    r = r - turns * 9.67653589793e-4
    z = r * r
    s = r + r * (z * horner(z, 2.63541936e-6, -1.98230239e-4, 8.33324557e-3, -1.66666661e-1))
    c = 1.0 + z * horner(
        z, -2.63066288e-7, 2.47750852e-5, -1.38886609e-3, 4.166666e-2, -0.5
    )
    return s, c, turns


def halves(x):
    high = x.astype(jnp.bfloat16)
    return high, (x - high.astype(jnp.float32)).astype(jnp.bfloat16)


def product(x, y):
    return jnp.dot(x, y, preferred_element_type=jnp.float32)

def finish_kernel(moved, found, recon, previous, shifted, slopes, commands, sems):
    copies = [
        pltpu.make_async_copy(moved.at[j], shifted.at[j], sems.at[j]) for j in range(moved.shape[0])
    ]
    copies.append(pltpu.make_async_copy(found, slopes, sems.at[moved.shape[0]]))
    for copy in copies:
        copy.start()
    commands[...] = 2.0 * recon[0, :] - previous[...]
    for copy in copies:
        copy.wait()


def finish(moved, found, recon, previous):
    shifted, slopes, commands = pl.pallas_call(
        finish_kernel,
        out_shape=tuple(
            jax.ShapeDtypeStruct(x.shape, jnp.float32) for x in (moved, found, previous)
        ),
        in_specs=[ANY, ANY, VMEM, VMEM],
        out_specs=(ANY, ANY, VMEM),
        scratch_shapes=[pltpu.SemaphoreType.DMA((moved.shape[0] + 1,))],
        compiler_params=pltpu.CompilerParams(vmem_limit_bytes=2**20),
        name="finish",
    )(moved, found, recon, previous)
    return shifted, jnp.transpose(slopes, (0, 2, 1, 3)), commands


def body(
    screens,
    layer_weight,
    wind_row,
    wind_col,
    foot_row,
    foot_col,
    frac_row,
    frac_col,
    amplitude,
    valid,
    recon_matrix,
    prev_recon,
):
    scalars = (layer_weight, wind_row, wind_col, foot_row, foot_col, frac_row, frac_col)
    moved, found, recon = frame(scalars, screens, amplitude, valid, recon_matrix)
    return finish(moved, found, recon, prev_recon)


def solution(mesh):
    return jax.shard_map(
        body,
        mesh=mesh,
        in_specs=(
            P(("runs", "layer"), "tile", None),
            P(("runs", "layer")),
            P("runs"),
            P("runs"),
            P(),
            P(),
            P(),
            P(),
            P("tile", "layer"),
            P("tile", "layer"),
            P("star", None, "tile", "layer", None),
            P("runs"),
        ),
        out_specs=(
            P(("runs", "layer"), "tile", None),
            P(("runs", "star"), None, "tile", "layer"),
            P("runs"),
        ),
        check_vma=False,
    )
```

time: 62.3 us -> 60 us (0.963)
  Pallas kernels: 61.5 us -> 59.2 us
    pallas_call x1, Pallas kernels: 59.7 us -> 57.4 us  [frame(): pl.pallas_call(functools.partial(frame_kernel, tiles, cores, blocks, star...]
where the time goes in v3:
time: 60 us; the launch traced here: 59.9 us
  Pallas kernels  59.2 us (99%)
  between operations  0.66 us (1%)
    pallas_call x1, Pallas kernels, frame(): pl.pallas_call(functools.partial(frame_kernel, tiles, cores, blocks, star...  57.4 us
    pallas_call x1, Pallas kernels, finish(): pl.pallas_call(finish_kernel, out_shape=tuple((jax.ShapeDtypeStruct(x.sha...  1.84 us

profile of v3, /device:TPU:0, one launch (start us, length us, event | category | flops | bytes accessed | tf_op | source)
XLA Modules:
  0.0 59.9 jit_solution(6308450671281149198)
XLA Ops:
  0.6 0.0 copy-start
  0.6 57.4 %frame.1 = (f32[3,96,1536]{2,1,0:T(8,128)S(1)}, f32[3,6,2,48]{3,2,1,0:T(2,128)S(1)}, f32[1,2688]{1,0:T(1,128)S(1)}) custom-call(f32[3]{0:T(128)} %weights_in.1, s32[6]{0:T(128)} %wind_row_in.1, s32[6]{0:T(128)} %wind_col_in.1, s32[6,6]{1,0:T(8,128)} %foot_row_in.1, s32[6,6]{1,0:T(8,128)} %foot_col_in.1, f32[6,6]{1,0:T(8,128)} %frac_row_in.1, ...), custom_call_target="tpu_custom_call" | custom-call | tf_op jit(solution)/shard_map/frame/pallas_call | solution.py:571
  58.0 0.0 copy-done
  58.0 1.8 %finish.1 = (f32[3,96,1536]{2,1,0:T(8,128)}, f32[3,6,2,48]{3,2,1,0:T(2,128)}, f32[2688]{0:T(1024)}) custom-call(f32[3,96,1536]{2,1,0:T(8,128)S(1)} %get-tuple-element.9.moved, f32[3,6,2,48]{3,2,1,0:T(2,128)S(1)} %get-tuple-element.10.found, f32[1,2688]{1,0:T(1,128)S(1)} %get-tuple-element.11.recon, f32[2688]{0:T(1024)S(1)} %copy-done), custom_call_target="tpu_custom_call" | custom-call | tf_op jit(solution)/shard_map/finish/pallas_call | solution.py:661
Async XLA Ops:
  0.6 57.4 %copy-start = (f32[2688]{0:T(1024)S(1)}, f32[2688]{0:T(1024)}, u32[]{:S(2)}) copy-start(f32[2688]{0:T(1024)} %previous.1) | copy-start | bytes 32260

commit v4 on v3

--- a/solution.py
+++ b/solution.py
@@ -14,7 +14,11 @@
 WIND = 4
 FOOT = 80
 LANES = 128
-HALO = -(-(WIND + FOOT + 1) // 8) * 8
+DEPTH = WIND + FOOT
+HALO = -(-DEPTH // 8) * 8
+DIRECT = DEPTH // 8 * 8
+EXTRA = DEPTH - DIRECT
+PACK = 8 // EXTRA
 MESH = pl.DeviceIdType.MESH
 ANY = pl.BlockSpec(memory_space=pl.ANY)
 HBM = pl.BlockSpec(memory_space=pltpu.HBM)
@@ -41,7 +45,7 @@
 def row_parts(rows):
     parts = 3 if (rows // PIX) % 3 == 0 else 1
     reach = WIND + FOOT + 1 - (rows // parts if parts > 1 else 0)
-    return parts, min(HALO, -(-reach // 8) * 8)
+    return parts, min(DIRECT, -(-reach // 8) * 8)
 
 
 def frame_kernel(
@@ -49,9 +53,9 @@
     frac_row_in, frac_col_in, screens, amplitude, valid, matrix, row_table, col_table, gather, spread,
     shifted, slopes, recon,
     weights, wind_row, wind_col, foot_row, foot_col, frac_row, frac_col,
-    field, land, outbox, inbox, share, amp, mask, weight, row_tab, col_tab, gath, spre,
+    field, land, rim, rim_land, outbox, inbox, share, amp, mask, weight, row_tab, col_tab, gath, spre,
     scale, amp_turned, real, stack, sums, total_terms, near, far,
-    zsend, zrecv, csend, crecv, xsend, xrecv, local, load, nsend, nrecv, fsend, frecv,
+    zsend, zrecv, csend, crecv, esend, erecv, fesend, ferecv, xsend, xrecv, local, load, nsend, nrecv, fsend, frecv,
 ):
     tile, core, layer = (lax.axis_index(n) for n in ("tile", "star", "layer"))
     up, down = lax.rem(tile + 1, tiles), lax.rem(tile + tiles - 1, tiles)
@@ -95,25 +99,54 @@
     greet(near_peers + far_peers)
     steps = strips // cores
     last = steps - 1
-    pieces = [(m, d, 0, HALO) for m in range(last) for d in range(2)]
-    near_rows = [(last, 0, HALO - inner, inner), (last, 1, 0, inner)]
-    far_rows = [(last, 0, 0, HALO - inner), (last, 1, inner, HALO - inner)]
+    pieces = [(m, d, 0, DIRECT) for m in range(last) for d in range(2)]
+    near_rows = [(last, 0, DIRECT - inner, inner), (last, 1, 0, inner)]
+    far_rows = [(last, 0, 0, DIRECT - inner), (last, 1, inner, DIRECT - inner)]
     far_rows = [p for p in far_rows if p[3]]
     pieces += near_rows + far_rows
+    targets = (up, down)
     sends = []
-    for q, (m, d, low, size) in enumerate(pieces):
+
+    def send(q):
+        m, d, low, size = pieces[q]
         n = m * cores + core
-        start, peer = ((rows - HALO, up), (0, down))[d]
         copy = pltpu.make_async_remote_copy(
-            src_ref=screens.at[:, pl.ds(start + low, size), column(n)],
+            src_ref=screens.at[:, pl.ds((rows - DIRECT, 0)[d] + low, size), column(n)],
             dst_ref=land.at[d, n, :, pl.ds(low, size), :],
             send_sem=zsend.at[q],
             recv_sem=zrecv.at[q],
-            device_id={"tile": peer},
+            device_id={"tile": targets[d]},
             device_id_type=MESH,
         )
         copy.start()
         sends.append(copy)
+
+    for q in range(2):
+        send(q)
+    for copy in copies:
+        copy.wait()
+    for d, start in enumerate((rows - DEPTH, DIRECT)):
+        for m in range(steps):
+            for j in range(lays):
+                e = m * lays + j
+                to = slice(e % PACK * EXTRA, (e % PACK + 1) * EXTRA)
+                rim[d, e // PACK, to, :] = field[
+                    j, m * cores + core, HALO + start : HALO + start + EXTRA, :
+                ]
+    rims = []
+    for d in range(2):
+        copy = pltpu.make_async_remote_copy(
+            src_ref=rim.at[d],
+            dst_ref=rim_land.at[d, core],
+            send_sem=esend.at[d],
+            recv_sem=erecv.at[d],
+            device_id={"tile": targets[d]},
+            device_id_type=MESH,
+        )
+        copy.start()
+        rims.append(copy)
+    for q in range(2, len(pieces)):
+        send(q)
     loads = []
     for n, (source, target) in enumerate(
         ((amplitude, amp), (valid, mask), (row_table, row_tab), (col_table, col_tab),
@@ -176,8 +209,6 @@
                     scale[w, p, at : at + part_subs, :] = ratio[
                         p * part_subs : (p + 1) * part_subs
                     ]
-    for copy in copies:
-        copy.wait()
     lane = lax.broadcasted_iota(jnp.int32, (8, LANES), 1)
 
     def window(j, row, base, n):
@@ -391,12 +422,39 @@
                 forward.wait_recv()
                 forwards.append(forward)
             m, d, low, size = pieces[q]
-            base = low + d * (HALO + rows)
+            base = low + (HALO - DIRECT, HALO + rows)[d]
             for n in range(m * cores, (m + 1) * cores):
                 for to in (n, n + strips):
                     if to < strips + 2:
                         for j in range(lays):
                             field[j, to, base : base + size, :] = land[d, n, j, low : low + size, :]
+
+    def take_rims():
+        for d in range(2):
+            rims[d].wait_recv()
+            for k, p in enumerate(partners):
+                forward = pltpu.make_async_remote_copy(
+                    src_ref=rim_land.at[d, core],
+                    dst_ref=rim_land.at[d, core],
+                    send_sem=fesend.at[d, k],
+                    recv_sem=ferecv.at[d, k],
+                    device_id={"star": p},
+                    device_id_type=MESH,
+                )
+                forward.start()
+                forwards.append(forward)
+        for forward in forwards[-2 * len(partners) :]:
+            forward.wait_recv()
+        for d, base in enumerate((HALO - DEPTH, HALO + rows + DIRECT)):
+            for m in range(steps):
+                for j in range(lays):
+                    e = m * lays + j
+                    at = slice(e % PACK * EXTRA, (e % PACK + 1) * EXTRA)
+                    for c in range(cores):
+                        n = m * cores + c
+                        for to in (n, n + strips):
+                            if to < strips + 2:
+                                field[j, to, base : base + EXTRA, :] = rim_land[d, c, e // PACK, at, :]
 
     def own(u, chosen, unroll=1):
         k, w = divmod(u, units)
@@ -413,6 +471,7 @@
         send_on([2 * m, 2 * m + 1])
         take([2 * m, 2 * m + 1])
         if m == 0:
+            take_rims()
             fetch_matrix()
         have = (m + 1) * cores
         while done < units * blocks and done * unit + unit + 2 <= have:
@@ -491,7 +550,7 @@
         )
         copy.start()
         far_copies.append(copy)
-    for copy in sends + forwards + swaps + near_copies:
+    for copy in sends + rims + forwards + swaps + near_copies:
         copy.wait_send()
     for copy in far_copies:
         copy.wait()
@@ -561,7 +620,8 @@
     while slots * part_subs % 8:
         slots += 1
     lanes = 2 * slots * part_subs * depth
-    pieces = 2 * (strips // cores) + (2 if inner < HALO else 0)
+    pieces = 2 * (strips // cores) + (2 if inner < DIRECT else 0)
+    rim_tiles = -(-(strips // cores) * lays // PACK)
     block = 2 * LANES if width % (2 * LANES) == 0 else LANES
     consts = tables(block, stars * part_subs, taps, depth, chunks, lanes)
     count = blocks * cores
@@ -580,7 +640,9 @@
         scratch_shapes=[pltpu.SMEM(t.shape, t.dtype) for t in scalars]
         + [
             pltpu.VMEM((lays, strips + 2, rows + 2 * HALO, LANES), f32),
-            pltpu.VMEM((2, strips, lays, HALO, LANES), f32),
+            pltpu.VMEM((2, strips, lays, DIRECT, LANES), f32),
+            pltpu.VMEM((2, rim_tiles, 8, LANES), f32),
+            pltpu.VMEM((2, cores, rim_tiles, 8, LANES), f32),
             pltpu.VMEM((units * (blocks - 1),) + piece, f32),
             pltpu.VMEM((blocks - 1, units) + piece, f32),
             pltpu.VMEM((units,) + piece, f32),
@@ -602,6 +664,10 @@
             dma((pieces,)),
             dma((pieces, cores - 1)),
             dma((pieces, cores - 1)),
+            dma((2,)),
+            dma((2,)),
+            dma((2, cores - 1)),
+            dma((2, cores - 1)),
             dma((units * (blocks - 1),)),
             dma((units * (blocks - 1),)),
             dma((strips + 2,)),

time: 60 us -> 59 us (0.983)
  Pallas kernels: 59.2 us -> 58.2 us
    pallas_call x1, Pallas kernels: 57.4 us -> 56.3 us  [frame(): pl.pallas_call(functools.partial(frame_kernel, tiles, cores, blocks, star...]
where the time goes in v4:
time: 59 us; the launch traced here: 58.8 us
  Pallas kernels  58.2 us (99%)
  between operations  0.66 us (1%)
    pallas_call x1, Pallas kernels, frame(): pl.pallas_call(functools.partial(frame_kernel, tiles, cores, blocks, star...  56.3 us
    pallas_call x1, Pallas kernels, finish(): pl.pallas_call(finish_kernel, out_shape=tuple((jax.ShapeDtypeStruct(x.sha...  1.84 us

profile of v4, /device:TPU:0, one launch (start us, length us, event | category | flops | bytes accessed | tf_op | source)
XLA Modules:
  0.0 58.8 jit_solution(3177612390287329731)
XLA Ops:
  0.6 0.0 copy-start
  0.6 56.3 %frame.1 = (f32[3,96,1536]{2,1,0:T(8,128)S(1)}, f32[3,6,2,48]{3,2,1,0:T(2,128)S(1)}, f32[1,2688]{1,0:T(1,128)S(1)}) custom-call(f32[3]{0:T(128)} %weights_in.1, s32[6]{0:T(128)} %wind_row_in.1, s32[6]{0:T(128)} %wind_col_in.1, s32[6,6]{1,0:T(8,128)} %foot_row_in.1, s32[6,6]{1,0:T(8,128)} %foot_col_in.1, f32[6,6]{1,0:T(8,128)} %frac_row_in.1, ...), custom_call_target="tpu_custom_call" | custom-call | tf_op jit(solution)/shard_map/frame/pallas_call | solution.py:631
  57.0 0.0 copy-done
  57.0 1.8 %finish.1 = (f32[3,96,1536]{2,1,0:T(8,128)}, f32[3,6,2,48]{3,2,1,0:T(2,128)}, f32[2688]{0:T(1024)}) custom-call(f32[3,96,1536]{2,1,0:T(8,128)S(1)} %get-tuple-element.9.moved, f32[3,6,2,48]{3,2,1,0:T(2,128)S(1)} %get-tuple-element.10.found, f32[1,2688]{1,0:T(1,128)S(1)} %get-tuple-element.11.recon, f32[2688]{0:T(1024)S(1)} %copy-done), custom_call_target="tpu_custom_call" | custom-call | tf_op jit(solution)/shard_map/finish/pallas_call | solution.py:727
Async XLA Ops:
  0.6 56.4 %copy-start = (f32[2688]{0:T(1024)S(1)}, f32[2688]{0:T(1024)}, u32[]{:S(2)}) copy-start(f32[2688]{0:T(1024)} %previous.1) | copy-start | bytes 32260

commit v5 on v4

--- a/solution.py
+++ b/solution.py
@@ -26,11 +26,15 @@
 VMEM = pl.BlockSpec(memory_space=pltpu.VMEM)
 
 
+def signal(sem, peer):
+    pl.semaphore_signal(sem, inc=1, device_id=peer, device_id_type=MESH)
+
+
 def greet(peers):
     barrier = pltpu.get_barrier_semaphore()
     for peer in peers:
-        pl.semaphore_signal(barrier, inc=1, device_id=peer, device_id_type=MESH)
-    pl.semaphore_wait(barrier, len(peers))
+        signal(barrier, peer)
+    return lambda: pl.semaphore_wait(barrier, len(peers))
 
 
 def plan(rows, cols, blocks):
@@ -42,10 +46,13 @@
     return strips, per_block, unit, units, group
 
 
-def row_parts(rows):
+def row_parts(rows, cols, blocks, cores):
     parts = 3 if (rows // PIX) % 3 == 0 else 1
-    reach = WIND + FOOT + 1 - (rows // parts if parts > 1 else 0)
-    return parts, min(DIRECT, -(-reach // 8) * 8)
+    inner = min(DIRECT, -(-(DEPTH - rows // parts) // 8) * 8) if parts > 1 else DIRECT
+    strips, _, unit, units, group = plan(rows, cols, blocks)
+    ready = ((strips // cores - 2) * cores - 2) // unit
+    split = 0 < inner < DIRECT and group == 1 and units * (blocks - 1) <= ready
+    return parts, inner, split
 
 
 def frame_kernel(
@@ -73,7 +80,7 @@
     chunks = units // group
     width = group * unit * LANES
     subs = rows // PIX
-    parts, inner = row_parts(rows)
+    parts, inner, split = row_parts(rows, cols, blocks, cores)
     part_rows, part_subs = rows // parts, subs // parts
     first = (layer + 1) * per_block + strips - 1
     star_start, layer_start = core * stars, layer * lays
@@ -87,6 +94,7 @@
         start = pl.multiple_of(lax.rem(first + n, strips) * LANES, LANES)
         return pl.ds(start, size * LANES)
 
+    greeted = greet(near_peers + far_peers)
     copies = []
     for n in range(strips + 2):
         copy = pltpu.make_async_copy(
@@ -96,14 +104,13 @@
         )
         copy.start()
         copies.append(copy)
-    greet(near_peers + far_peers)
+    greeted()
     steps = strips // cores
-    last = steps - 1
-    pieces = [(m, d, 0, DIRECT) for m in range(last) for d in range(2)]
-    near_rows = [(last, 0, DIRECT - inner, inner), (last, 1, 0, inner)]
-    far_rows = [(last, 0, 0, DIRECT - inner), (last, 1, inner, DIRECT - inner)]
-    far_rows = [p for p in far_rows if p[3]]
-    pieces += near_rows + far_rows
+    full = steps - 2 if split else steps
+    pieces = [(m, d, 0, DIRECT) for m in range(full) for d in range(2)]
+    for m in range(full, steps):
+        pieces += [(m, 0, DIRECT - inner, inner), (m, 1, 0, inner)]
+        pieces += [(m, 0, 0, DIRECT - inner), (m, 1, inner, DIRECT - inner)]
     targets = (up, down)
     sends = []
 
@@ -118,11 +125,11 @@
             device_id={"tile": targets[d]},
             device_id_type=MESH,
         )
-        copy.start()
         sends.append(copy)
+        return copy
 
     for q in range(2):
-        send(q)
+        send(q).start()
     for copy in copies:
         copy.wait()
     for d, start in enumerate((rows - DEPTH, DIRECT)):
@@ -146,7 +153,7 @@
         copy.start()
         rims.append(copy)
     for q in range(2, len(pieces)):
-        send(q)
+        send(q).start()
     loads = []
     for n, (source, target) in enumerate(
         ((amplitude, amp), (valid, mask), (row_table, row_tab), (col_table, col_tab),
@@ -467,56 +474,80 @@
 
     whole = list(range(parts))
     done = 0
-    for m in range(last):
-        send_on([2 * m, 2 * m + 1])
-        take([2 * m, 2 * m + 1])
+    def pair(n):
+        return [2 * n, 2 * n + 1]
+
+    def finish_unit(u):
+        k, w = divmod(u, units)
+        if k < blocks - 1:
+            compute(u, to_outbox(u), whole)
+            copy = pltpu.make_async_remote_copy(
+                src_ref=outbox.at[u],
+                dst_ref=inbox.at[k, w],
+                send_sem=xsend.at[u],
+                recv_sem=xrecv.at[u],
+                device_id={"layer": peers[k]},
+                device_id_type=MESH,
+            )
+            copy.start()
+            swaps.append(copy)
+        else:
+            own(u, whole)
+            arrived(w)
+            if (w + 1) % group == 0:
+                slope_all([w // group], whole)
+
+    def slope_all(chosen, some):
+        project(slope_parts([(c, p) for c in chosen for p in some]))
+
+    late = []
+    for m in range(full):
+        send_on(pair(m))
+        take(pair(m))
         if m == 0:
             take_rims()
             fetch_matrix()
         have = (m + 1) * cores
-        while done < units * blocks and done * unit + unit + 2 <= have:
-            k, w = divmod(done, units)
-            if k < blocks - 1:
-                compute(done, to_outbox(done), whole)
-                copy = pltpu.make_async_remote_copy(
-                    src_ref=outbox.at[done],
-                    dst_ref=inbox.at[k, w],
-                    send_sem=xsend.at[done],
-                    recv_sem=xrecv.at[done],
-                    device_id={"layer": peers[k]},
-                    device_id_type=MESH,
-                )
-                copy.start()
-                swaps.append(copy)
+        while done < units * blocks and (
+            have == strips or done * unit + unit + 2 <= have
+        ):
+            finish_unit(done)
+            if have < strips:
+                move(done)
             else:
-                own(done, whole)
-                arrived(w)
-                if (w + 1) % group == 0:
-                    c = w // group
-                    project(slope_parts([(c, p) for p in whole]))
-            move(done)
+                late.append(done)
             done += 1
-    late = list(range(done, units * blocks))
-    late_chunks = sorted({(u % units) // group for u in late})
-    split = last * 2 + 2 < len(pieces)
-    send_on([2 * last, 2 * last + 1])
-    take([2 * last, 2 * last + 1])
     if split:
-        outer = [2 * last + 2, 2 * last + 3]
-        middle = whole[1:-1]
+        middle, rest = whole[1:-1], [whole[0], whole[-1]]
+        have = (steps - 1) * cores
+        soon = [u for u in range(done, units * blocks) if u * unit + unit + 2 <= have]
+        late = [u for u in range(done, units * blocks) if u not in soon]
+        soon_chunks, late_chunks = ([u % units for u in some] for some in (soon, late))
+        near_soon, far_soon, near_late, far_late = (pair(full + n) for n in range(4))
+        send_on(near_soon)
+        take(near_soon)
+        for u in soon:
+            own(u, middle, True)
+            arrived(u % units)
+        slope_all(soon_chunks, middle)
+        send_on(far_soon)
+        take(far_soon)
+        for u in soon:
+            own(u, rest, True)
+        slope_all(soon_chunks, rest)
+        send_on(near_late)
+        for u in soon:
+            move(u)
+        take(near_late)
         for u in late:
             own(u, middle, True)
             arrived(u % units)
-        terms = slope_parts([(c, p) for c in late_chunks for p in middle])
-        send_on(outer)
-        project(terms)
-        take(outer)
-    rest = [whole[0], whole[-1]] if split else whole
-    for u in late:
-        own(u, rest, True)
-        if not split:
-            arrived(u % units)
-    project(slope_parts([(c, p) for c in late_chunks for p in rest]))
+        send_on(far_late)
+        slope_all(late_chunks, middle)
+        take(far_late)
+        for u in late:
+            own(u, rest, True)
+        slope_all(late_chunks, rest)
     near_copies = []
     for k, peer in enumerate(near_peers):
         copy = pltpu.make_async_remote_copy(
@@ -539,13 +570,14 @@
         total = total + near[k]
     far[tile] = total
     far_copies = []
-    for k, peer in enumerate(far_peers):
+    toward = jnp.where(2 * tile < tiles, 1, tiles - 1)
+    for k in range(tiles - 1, 0, -1):
         copy = pltpu.make_async_remote_copy(
             src_ref=far.at[tile],
             dst_ref=far.at[tile],
-            send_sem=fsend.at[k],
-            recv_sem=frecv.at[k],
-            device_id=peer,
+            send_sem=fsend.at[k - 1],
+            recv_sem=frecv.at[tile],
+            device_id={"tile": lax.rem(tile + toward * k, tiles)},
             device_id_type=MESH,
         )
         copy.start()
@@ -553,7 +585,17 @@
     for copy in sends + rims + forwards + swaps + near_copies:
         copy.wait_send()
     for copy in far_copies:
-        copy.wait()
+        copy.wait_send()
+    for k in range(1, tiles):
+        source = lax.rem(tile + k, tiles)
+        pltpu.make_async_remote_copy(
+            src_ref=far.at[source],
+            dst_ref=far.at[source],
+            send_sem=fsend.at[k - 1],
+            recv_sem=frecv.at[source],
+            device_id={"tile": source},
+            device_id_type=MESH,
+        ).wait_recv()
     total = far[0]
     for k in range(1, tiles):
         total = total + far[k]
@@ -614,13 +656,13 @@
     width = group * unit * LANES
     taps = sub_cols // chunks
     depth = -(-taps // 16) * 16
-    parts, inner = row_parts(rows)
+    parts, inner, split = row_parts(rows, cols, blocks, cores)
     part_subs = subs // parts
     slots = stars
     while slots * part_subs % 8:
         slots += 1
     lanes = 2 * slots * part_subs * depth
-    pieces = 2 * (strips // cores) + (2 if inner < DIRECT else 0)
+    pieces = 2 * (strips // cores) + (4 if split else 0)
     rim_tiles = -(-(strips // cores) * lays // PACK)
     block = 2 * LANES if width % (2 * LANES) == 0 else LANES
     consts = tables(block, stars * part_subs, taps, depth, chunks, lanes)
@@ -675,7 +717,7 @@
             dma((count - 1,)),
             dma((count - 1,)),
             dma((tiles - 1,)),
-            dma((tiles - 1,)),
+            dma((tiles,)),
         ],
         compiler_params=pltpu.CompilerParams(
             collective_id=0, has_side_effects=True, vmem_limit_bytes=48 * 2**20

time: 59 us -> 57.7 us (0.978)
  Pallas kernels: 58.2 us -> 56.9 us
    pallas_call x1, Pallas kernels: 56.3 us -> 55 us  [frame(): pl.pallas_call(functools.partial(frame_kernel, tiles, cores, blocks, star...]
where the time goes in v5:
time: 57.7 us; the launch traced here: 57.5 us
  Pallas kernels  56.9 us (99%)
  between operations  0.66 us (1%)
    pallas_call x1, Pallas kernels, frame(): pl.pallas_call(functools.partial(frame_kernel, tiles, cores, blocks, star...  55 us
    pallas_call x1, Pallas kernels, finish(): pl.pallas_call(finish_kernel, out_shape=tuple((jax.ShapeDtypeStruct(x.sha...  1.84 us

profile of v5, /device:TPU:0, one launch (start us, length us, event | category | flops | bytes accessed | tf_op | source)
XLA Modules:
  0.0 57.5 jit_solution(2492903800526979852)
XLA Ops:
  0.6 0.0 copy-start
  0.6 55.0 %frame.1 = (f32[3,96,1536]{2,1,0:T(8,128)S(1)}, f32[3,6,2,48]{3,2,1,0:T(2,128)S(1)}, f32[1,2688]{1,0:T(1,128)S(1)}) custom-call(f32[3]{0:T(128)} %weights_in.1, s32[6]{0:T(128)} %wind_row_in.1, s32[6]{0:T(128)} %wind_col_in.1, s32[6,6]{1,0:T(8,128)} %foot_row_in.1, s32[6,6]{1,0:T(8,128)} %foot_col_in.1, f32[6,6]{1,0:T(8,128)} %frac_row_in.1, ...), custom_call_target="tpu_custom_call" | custom-call | tf_op jit(solution)/shard_map/frame/pallas_call | solution.py:673
  55.7 0.0 copy-done
  55.7 1.8 %finish.1 = (f32[3,96,1536]{2,1,0:T(8,128)}, f32[3,6,2,48]{3,2,1,0:T(2,128)}, f32[2688]{0:T(1024)}) custom-call(f32[3,96,1536]{2,1,0:T(8,128)S(1)} %get-tuple-element.9.moved, f32[3,6,2,48]{3,2,1,0:T(2,128)S(1)} %get-tuple-element.10.found, f32[1,2688]{1,0:T(1,128)S(1)} %get-tuple-element.11.recon, f32[2688]{0:T(1024)S(1)} %copy-done), custom_call_target="tpu_custom_call" | custom-call | tf_op jit(solution)/shard_map/finish/pallas_call | solution.py:769
Async XLA Ops:
  0.6 55.1 %copy-start = (f32[2688]{0:T(1024)S(1)}, f32[2688]{0:T(1024)}, u32[]{:S(2)}) copy-start(f32[2688]{0:T(1024)} %previous.1) | copy-start | bytes 32260

commit v6 on v5

--- a/solution.py
+++ b/solution.py
@@ -57,10 +57,10 @@
 
 def frame_kernel(
     tiles, cores, blocks, stars, weights_in, wind_row_in, wind_col_in, foot_row_in, foot_col_in,
-    frac_row_in, frac_col_in, screens, amplitude, valid, matrix, row_table, col_table, gather, spread,
-    shifted, slopes, recon,
+    frac_row_in, frac_col_in, screens, amplitude, valid, previous, matrix, row_table, col_table, gather, spread,
+    shifted, slopes, commands,
     weights, wind_row, wind_col, foot_row, foot_col, frac_row, frac_col,
-    field, land, rim, rim_land, outbox, inbox, share, amp, mask, weight, row_tab, col_tab, gath, spre,
+    field, land, rim, rim_land, outbox, inbox, share, amp, mask, before, weight, row_tab, col_tab, gath, spre,
     scale, amp_turned, real, stack, sums, total_terms, near, far,
     zsend, zrecv, csend, crecv, esend, erecv, fesend, ferecv, xsend, xrecv, local, load, nsend, nrecv, fsend, frecv,
 ):
@@ -157,7 +157,7 @@
     loads = []
     for n, (source, target) in enumerate(
         ((amplitude, amp), (valid, mask), (row_table, row_tab), (col_table, col_tab),
-         (gather, gath), (spread, spre), (weights_in, weights), (wind_row_in, wind_row),
+         (gather, gath), (spread, spre), (previous, before), (weights_in, weights), (wind_row_in, wind_row),
          (wind_col_in, wind_col), (foot_row_in, foot_row), (foot_col_in, foot_col),
          (frac_row_in, frac_row), (frac_col_in, frac_col))
     ):
@@ -599,7 +599,7 @@
     total = far[0]
     for k in range(1, tiles):
         total = total + far[k]
-    recon[...] = total
+    commands[...] = 2.0 * total[0, :] - before[...]
 
 
 def tables(block, block_subs, taps, depth, chunks, lanes):
@@ -647,7 +647,7 @@
     return [pltpu.with_memory_space_constraint(x, pltpu.HBM) for x in arrays]
 
 
-def frame(scalars, screens, amplitude, valid, matrix):
+def frame(scalars, screens, amplitude, valid, previous, matrix):
     tiles, blocks, cores = (lax.axis_size(n) for n in ("tile", "layer", "star"))
     lays, rows, cols = screens.shape
     stars, _, subs, sub_cols, commands = matrix.shape
@@ -675,9 +675,9 @@
         out_shape=(
             pltpu.VMEM((lays, rows, cols), f32),
             pltpu.VMEM((stars, subs, 2, sub_cols), f32),
-            pltpu.VMEM((1, commands), f32),
+            pltpu.VMEM((commands,), f32),
         ),
-        in_specs=[HBM] * (len(scalars) + 4 + len(consts)),
+        in_specs=[HBM] * (len(scalars) + 5 + len(consts)),
         out_specs=(VMEM, VMEM, VMEM),
         scratch_shapes=[pltpu.SMEM(t.shape, t.dtype) for t in scalars]
         + [
@@ -690,6 +690,7 @@
             pltpu.VMEM((units,) + piece, f32),
             pltpu.VMEM(amplitude.shape, f32),
             pltpu.VMEM(valid.shape, valid.dtype),
+            pltpu.VMEM(previous.shape, f32),
             pltpu.VMEM((chunks, parts, 2, slots, part_subs, depth, commands), bf16),
         ]
         + [pltpu.VMEM(t.shape, bf16) for t in consts]
@@ -713,7 +714,7 @@
             dma((units * (blocks - 1),)),
             dma((units * (blocks - 1),)),
             dma((strips + 2,)),
-            dma((6 + len(scalars) + chunks * parts * 2,)),
+            dma((7 + len(scalars) + chunks * parts * 2,)),
             dma((count - 1,)),
             dma((count - 1,)),
             dma((tiles - 1,)),
@@ -723,7 +724,7 @@
             collective_id=0, has_side_effects=True, vmem_limit_bytes=48 * 2**20
         ),
         name="frame",
-    )(*stay(*scalars, screens, amplitude, valid, matrix, *consts))
+    )(*stay(*scalars, screens, amplitude, valid, previous, matrix, *consts))
 
 
 def horner(z, first, *rest):
@@ -753,31 +754,26 @@
 def product(x, y):
     return jnp.dot(x, y, preferred_element_type=jnp.float32)
 
-def finish_kernel(moved, found, recon, previous, shifted, slopes, commands, sems):
-    copies = [
-        pltpu.make_async_copy(moved.at[j], shifted.at[j], sems.at[j]) for j in range(moved.shape[0])
-    ]
-    copies.append(pltpu.make_async_copy(found, slopes, sems.at[moved.shape[0]]))
-    for copy in copies:
-        copy.start()
-    commands[...] = 2.0 * recon[0, :] - previous[...]
+def finish_kernel(*refs):
+    sems, count = refs[-1], len(refs) // 2
+    copies = []
+    for n in range(count):
+        copies.append(pltpu.make_async_copy(refs[n], refs[count + n], sems.at[n]))
+        copies[-1].start()
     for copy in copies:
         copy.wait()
 
 
-def finish(moved, found, recon, previous):
-    shifted, slopes, commands = pl.pallas_call(
+def finish(*arrays):
+    return pl.pallas_call(
         finish_kernel,
-        out_shape=tuple(
-            jax.ShapeDtypeStruct(x.shape, jnp.float32) for x in (moved, found, previous)
-        ),
-        in_specs=[ANY, ANY, VMEM, VMEM],
-        out_specs=(ANY, ANY, VMEM),
-        scratch_shapes=[pltpu.SemaphoreType.DMA((moved.shape[0] + 1,))],
+        out_shape=[jax.ShapeDtypeStruct(x.shape, x.dtype) for x in arrays],
+        in_specs=[ANY] * len(arrays),
+        out_specs=[ANY] * len(arrays),
+        scratch_shapes=[pltpu.SemaphoreType.DMA((len(arrays),))],
         compiler_params=pltpu.CompilerParams(vmem_limit_bytes=2**20),
         name="finish",
-    )(moved, found, recon, previous)
-    return shifted, jnp.transpose(slopes, (0, 2, 1, 3)), commands
+    )(*arrays)
 
 
 def body(
@@ -795,8 +791,10 @@
     prev_recon,
 ):
     scalars = (layer_weight, wind_row, wind_col, foot_row, foot_col, frac_row, frac_col)
-    moved, found, recon = frame(scalars, screens, amplitude, valid, recon_matrix)
-    return finish(moved, found, recon, prev_recon)
+    shifted, slopes, commands = finish(
+        *frame(scalars, screens, amplitude, valid, prev_recon, recon_matrix)
+    )
+    return shifted, jnp.transpose(slopes, (0, 2, 1, 3)), commands
 
 
 def solution(mesh):

time: 57.7 us -> 57.1 us (0.990)
  Pallas kernels: 56.9 us -> 56.3 us
    pallas_call x1, Pallas kernels: 1.84 us -> 1.24 us  [finish(): pl.pallas_call(finish_kernel, out_shape=[jax.ShapeDtypeStruct(x.shape, x....]
where the time goes in v6:
time: 57.1 us; the launch traced here: 56.9 us
  Pallas kernels  56.3 us (99%)
  between operations  0.64 us (1%)
    pallas_call x1, Pallas kernels, frame(): pl.pallas_call(functools.partial(frame_kernel, tiles, cores, blocks, star...  55 us
    pallas_call x1, Pallas kernels, finish(): pl.pallas_call(finish_kernel, out_shape=[jax.ShapeDtypeStruct(x.shape, x....  1.24 us

profile of v6, /device:TPU:0, one launch (start us, length us, event | category | flops | bytes accessed | tf_op | source)
XLA Modules:
  0.0 56.9 jit_solution(8166468313937385961)
XLA Ops:
  0.6 55.0 %frame.1 = (f32[3,96,1536]{2,1,0:T(8,128)S(1)}, f32[3,6,2,48]{3,2,1,0:T(2,128)S(1)}, f32[2688]{0:T(1024)S(1)}) custom-call(f32[3]{0:T(128)} %weights_in.1, s32[6]{0:T(128)} %wind_row_in.1, s32[6]{0:T(128)} %wind_col_in.1, s32[6,6]{1,0:T(8,128)} %foot_row_in.1, s32[6,6]{1,0:T(8,128)} %foot_col_in.1, f32[6,6]{1,0:T(8,128)} %frac_row_in.1, f32[6,6]{1,0:T(8,128)} %frac_col_in.1, ...), custom_call_target="tpu_custom_call" | custom-call | tf_op jit(solution)/shard_map/frame/pallas_call | solution.py:673
  55.7 1.2 %finish.1 = (f32[3,96,1536]{2,1,0:T(8,128)}, f32[3,6,2,48]{3,2,1,0:T(2,128)}, f32[2688]{0:T(1024)}) custom-call(f32[3,96,1536]{2,1,0:T(8,128)S(1)} %get-tuple-element.9.refs_0_, f32[3,6,2,48]{3,2,1,0:T(2,128)S(1)} %get-tuple-element.10.refs_1_, f32[2688]{0:T(1024)S(1)} %get-tuple-element.11.refs_2_), custom_call_target="tpu_custom_call" | custom-call | tf_op jit(solution)/shard_map/finish/pallas_call | solution.py:768

commit v7 on v6

--- a/solution.py
+++ b/solution.py
@@ -758,8 +758,16 @@
     sems, count = refs[-1], len(refs) // 2
     copies = []
     for n in range(count):
-        copies.append(pltpu.make_async_copy(refs[n], refs[count + n], sems.at[n]))
-        copies[-1].start()
+        source, target = refs[n], refs[count + n]
+        whole = n > 0
+        half = 0 if whole else source.shape[1] // 2
+        cuts = [None] if whole else [
+            (j, pl.ds(i * half, half)) for j in range(source.shape[0]) for i in range(2)
+        ]
+        for cut in cuts:
+            pair = (source, target) if whole else (source.at[cut], target.at[cut])
+            copies.append(pltpu.make_async_copy(*pair, sems.at[len(copies)]))
+            copies[-1].start()
     for copy in copies:
         copy.wait()
 
@@ -770,7 +778,7 @@
         out_shape=[jax.ShapeDtypeStruct(x.shape, x.dtype) for x in arrays],
         in_specs=[ANY] * len(arrays),
         out_specs=[ANY] * len(arrays),
-        scratch_shapes=[pltpu.SemaphoreType.DMA((len(arrays),))],
+        scratch_shapes=[pltpu.SemaphoreType.DMA((2 * arrays[0].shape[0] + len(arrays) - 1,))],
         compiler_params=pltpu.CompilerParams(vmem_limit_bytes=2**20),
         name="finish",
     )(*arrays)

time: 57.1 us -> 57.1 us (level)
  no operation moved by 1% of the time
where the time goes in v7:
time: 57.1 us; the launch traced here: 57 us
  Pallas kernels  56.3 us (99%)
  between operations  0.64 us (1%)
    pallas_call x1, Pallas kernels, frame(): pl.pallas_call(functools.partial(frame_kernel, tiles, cores, blocks, star...  55.1 us
    pallas_call x1, Pallas kernels, finish(): pl.pallas_call(finish_kernel, out_shape=[jax.ShapeDtypeStruct(x.shape, x....  1.28 us

profile of v7, /device:TPU:0, one launch (start us, length us, event | category | flops | bytes accessed | tf_op | source)
XLA Modules:
  0.0 57.0 jit_solution(2499239669571739969)
XLA Ops:
  0.6 55.1 %frame.1 = (f32[3,96,1536]{2,1,0:T(8,128)S(1)}, f32[3,6,2,48]{3,2,1,0:T(2,128)S(1)}, f32[2688]{0:T(1024)S(1)}) custom-call(f32[3]{0:T(128)} %weights_in.1, s32[6]{0:T(128)} %wind_row_in.1, s32[6]{0:T(128)} %wind_col_in.1, s32[6,6]{1,0:T(8,128)} %foot_row_in.1, s32[6,6]{1,0:T(8,128)} %foot_col_in.1, f32[6,6]{1,0:T(8,128)} %frac_row_in.1, f32[6,6]{1,0:T(8,128)} %frac_col_in.1, ...), custom_call_target="tpu_custom_call" | custom-call | tf_op jit(solution)/shard_map/frame/pallas_call | solution.py:673
  55.7 1.3 %finish.1 = (f32[3,96,1536]{2,1,0:T(8,128)}, f32[3,6,2,48]{3,2,1,0:T(2,128)}, f32[2688]{0:T(1024)}) custom-call(f32[3,96,1536]{2,1,0:T(8,128)S(1)} %get-tuple-element.9.refs_0_, f32[3,6,2,48]{3,2,1,0:T(2,128)S(1)} %get-tuple-element.10.refs_1_, f32[2688]{0:T(1024)S(1)} %get-tuple-element.11.refs_2_), custom_call_target="tpu_custom_call" | custom-call | tf_op jit(solution)/shard_map/finish/pallas_call | solution.py:776
